TPU v7x, 512 devices: a whole 4x4x16 slice. The times are simulated.
512 devices in a mesh: row: 32 (over z, core), col: 16 (over y, x).
Axes of the slice: x: 4, y: 4, z: 16, core: 2. Of those that a mesh axis runs over, the one named last changes fastest.
Arguments:
- panel: float32 [16384, 256], P('row'), may hold values from -4 to 132
- trailing: float32 [16384, 16384], P('row', 'col'), may hold values from -6 to 6, as said below
Outputs:
- band_block: float32 [256, 256], replicated
- updated: float32 [16384, 16384], P('row', 'col')
Inputs may be any that keep to these rules, and one draw needn't show every extreme that they name: trailing equals its own transpose.
All inputs are finite; a program needn't handle non-finite values.
Results may differ from a plain program's by a relative error of at most 0.000086.
Values sent between devices are 32-bit elements; how exact they have to be, the bound alone decides.
No kernel may reach another device: no remote copies, remote signals or barrier semaphores. Data moves between devices by JAX's collectives and lax.ppermute only.
A program may use at most 64 MiB of HBM per device.

v0:
```python
import jax
import jax.numpy as jnp
from jax import lax
from jax.sharding import PartitionSpec as P

highest = lax.Precision.HIGHEST


def from_root(value, axis, root):
    mine = lax.axis_index(axis) == root
    return lax.psum(jnp.where(mine, value, jnp.zeros_like(value)), axis)


def product(left, right):
    return jnp.dot(left, right, precision=highest, preferred_element_type=jnp.float32)


def product_nt(left, right):
    return lax.dot_general(
        left, right, (((1,), (1,)), ((), ())), precision=highest, preferred_element_type=jnp.float32
    )


def product_tn(left, right):
    return lax.dot_general(
        left, right, (((0,), (0,)), ((), ())), precision=highest, preferred_element_type=jnp.float32
    )


def reflector_inverse(top_basis):
    size = top_basis.shape[0]
    shifted = jnp.eye(size, dtype=jnp.float32) + top_basis.T
    normal_eq = product_tn(shifted, shifted)
    chol_factor = jnp.linalg.cholesky(normal_eq)
    return jax.scipy.linalg.cho_solve((chol_factor, True), shifted.T)


def unit_rows(count, width, start):
    rows_here = start + lax.broadcasted_iota(jnp.int32, (count, width), 0)
    cols_here = lax.broadcasted_iota(jnp.int32, (count, width), 1)
    return (rows_here == cols_here).astype(jnp.float32)


def body(panel, trailing):
    row_count, width = panel.shape
    groups = lax.axis_size("row") // lax.axis_size("col")
    row_index = lax.axis_index("row")
    col_index = lax.axis_index("col")
    on_top = (row_index == 0).astype(jnp.float32)
    top_panel = panel[:width] * on_top
    gram, top_panel = lax.psum((product_tn(panel, panel), top_panel), "row")
    factor = jnp.linalg.cholesky(gram)
    band_block = -factor.T
    ortho_rows = jax.scipy.linalg.solve_triangular(factor, panel.T, lower=True).T
    top_basis = jax.scipy.linalg.solve_triangular(factor, top_panel.T, lower=True).T
    reflect_rows = ortho_rows + unit_rows(row_count, width, row_index * row_count)
    pieces = []
    for offset in range(groups):
        pieces.append(from_root(reflect_rows, "row", col_index * groups + offset))
    reflect_cols = jnp.concatenate(pieces, axis=0)
    inverse_top = reflector_inverse(top_basis)
    summed = lax.psum(product(trailing, reflect_cols), "col")
    projected = product_nt(summed, inverse_top)
    paired = lax.psum(product_tn(reflect_rows, projected), "row")
    coupling = product(inverse_top, paired)
    correction = projected - 0.5 * product(reflect_rows, coupling)
    pieces = []
    for offset in range(groups):
        pieces.append(from_root(correction, "row", col_index * groups + offset))
    correction_cols = jnp.concatenate(pieces, axis=0)
    updated = (
        trailing - product_nt(reflect_rows, correction_cols) - product_nt(correction, reflect_cols)
    )
    return (band_block, updated)


def solution(mesh):
    in_specs = (P("row", None), P("row", "col"))
    out_specs = (P(), P("row", "col"))
    return jax.shard_map(body, mesh=mesh, in_specs=in_specs, out_specs=out_specs, check_vma=False)
```

profile of v0, /device:TPU:1, one launch (start us, length us, event | category | flops | bytes accessed | tf_op | source)
XLA Modules:
  0.0 1127.1 jit_solution(10523376161011979055)
XLA Ops:
  7.2 2.9 fusion.44
  10.2 1.7 multiply_bitcast_fusion
  11.9 210.5 %all-reduce.9.cloned.1.call-done = f32[256,256]{0,1:T(8,128)} async-done(((f32[256,256]{0,1:T(8,128)}), f32[256,256]{0,1:T(8,128)}) %all-reduce.9.cloned.1.call-update) | async-done | bytes 262160 | tf_op jit(solution)/shard_map/psum | solution.py:51
  222.4 1.1 copy.5
  223.5 1.0 fusion.9
  224.5 11.7 %cholesky.130 = f32[128,128]{1,0:T(8,128)S(1)} custom-call(f32[128,128]{1,0:T(8,128)S(1)} %cholesky.194), custom_call_target="Cholesky" | custom-call | tf_op jit(solution)/shard_map/jit(cholesky)/cholesky | solution.py:52
  236.3 9.8 custom-call.23
  246.1 0.2 constant_dynamic-update-slice_fusion.5
  246.3 0.3 convolution_subtract_fusion.5
  246.6 11.7 %cholesky.147 = f32[128,128]{1,0:T(8,128)S(1)} custom-call(f32[128,128]{1,0:T(8,128)S(1)} %convolution_subtract_fusion.5), custom_call_target="Cholesky" | custom-call | tf_op jit(solution)/shard_map/jit(cholesky)/cholesky | solution.py:52
  258.3 0.6 compare_reduce_fusion.2
  260.3 0.8 fusion.10
  261.1 4.5 while.6
  261.6 0.6 fusion.70
  262.2 1.4 bitcast_dynamic-update-slice_fusion.4
  263.6 0.6 fusion.70
  264.2 1.4 bitcast_dynamic-update-slice_fusion.4
  265.6 19.7 %custom-call.19 = f32[2,128,128]{1,2,0:T(8,128)S(1)} custom-call(f32[2,128,128]{2,1,0:T(8,128)S(1)} %get-tuple-element.19), custom_call_target="InvertDiagBlocksLowerTriangular" | custom-call | tf_op jit(solution)/shard_map/jit(_solve_triangular)/triangular_solve | solution.py:54
  285.3 0.4 fusion.6
  285.7 0.6 convolution_subtract_fusion
  286.3 0.4 fusion.26
  286.8 0.7 copy-done.1
  287.5 1.1 broadcast_select_fusion.2
  288.6 212.1 %all-reduce.17.cloned.1.call-done = (f32[512,256]{0,1:T(8,128)}, f32[512,256]{0,1:T(8,128)}, f32[256,256]{0,1:T(8,128)}) async-done(((f32[512,256]{0,1:T(8,128)}, f32[512,256]{0,1:T(8,128)}, f32[256,256]{0,1:T(8,128)}), (f32[512,256]{0,1:T(8,128)}, f32[512,256]{0,1:T(8,128)}, f32[256,256]{0,1:T(8,128)})) %all-reduce.17.cloned.1.call-update) | async-done | bytes 1310736 | tf_op jit(solution)/shard_map/psum | solution.py:11
  500.8 1.2 fusion.17
  502.0 1.3 convolution_subtract_fusion.3
  503.3 0.3 fusion.25
  503.6 0.6 fusion.14
  504.2 0.1 copy.6
  504.4 11.7 %cholesky.164 = f32[128,128]{1,0:T(8,128)S(1)} custom-call(f32[128,128]{1,0:T(8,128)S(1)} %cholesky.197), custom_call_target="Cholesky" | custom-call | tf_op jit(solution)/shard_map/jit(cholesky)/cholesky | solution.py:34
  516.2 0.6 compare_reduce_fusion.1
  516.8 9.8 custom-call.25
  526.7 0.2 constant_dynamic-update-slice_fusion.2
  526.9 0.3 convolution_subtract_fusion.4
  527.1 11.7 %cholesky.181 = f32[128,128]{1,0:T(8,128)S(1)} custom-call(f32[128,128]{1,0:T(8,128)S(1)} %convolution_subtract_fusion.4), custom_call_target="Cholesky" | custom-call | tf_op jit(solution)/shard_map/jit(cholesky)/cholesky | solution.py:34
  538.9 0.6 compare_reduce_fusion
  540.9 4.2 while.7
  541.1 0.6 fusion.71
  541.7 1.4 bitcast_dynamic-update-slice_fusion.5
  543.1 0.6 fusion.71
  543.7 1.4 bitcast_dynamic-update-slice_fusion.5
  545.1 19.7 %custom-call.20 = f32[2,128,128]{1,2,0:T(8,128)S(1)} custom-call(f32[2,128,128]{2,1,0:T(8,128)S(1)} %get-tuple-element.27), custom_call_target="InvertDiagBlocksLowerTriangular" | custom-call | tf_op jit(solution)/shard_map/jit(_cho_solve)/triangular_solve | solution.py:35
  564.8 0.3 fusion.15
  565.1 0.4 convolution_subtract_fusion.2
  565.5 1.0 fusion.28
  566.5 1.1 constant_dynamic-update-slice_fusion.1
  567.6 1.1 constant_dynamic-update-slice_fusion
  568.7 2.7 convolution_bitcast_fusion
  571.5 1.2 fusion.29
  572.7 1.3 convolution_subtract_fusion.1
  574.0 1.8 fusion.27
  575.7 110.3 %all-reduce.11.cloned.1.call-done = f32[512,256]{0,1:T(8,128)} async-done(((f32[512,256]{0,1:T(8,128)}), f32[512,256]{0,1:T(8,128)}) %all-reduce.11.cloned.1.call-update) | async-done | bytes 524304 | tf_op jit(solution)/shard_map/psum | solution.py:62
  686.0 2.1 fusion.12
  688.1 0.8 copy-done.3
  688.9 2.3 fusion.40
  691.2 0.3 all-reduce.15.cloned.1.call-start
  691.4 2.0 copy.8
  693.5 204.8 %all-reduce.13.cloned.1.call-done = f32[256,256]{1,0:T(8,128)} async-done(((f32[256,256]{1,0:T(8,128)}), f32[256,256]{1,0:T(8,128)}) %all-reduce.13.cloned.1.call-update) | async-done | bytes 262160 | tf_op jit(solution)/shard_map/psum | solution.py:64
  898.3 1.4 fusion.11
  899.7 3.0 broadcast_select_fusion.1
  902.8 1.8 copy.9
  904.6 209.1 %all-reduce.15.cloned.1.call-done = (f32[512,256]{0,1:T(8,128)}, f32[512,256]{0,1:T(8,128)}) async-done(((f32[512,256]{0,1:T(8,128)}, f32[512,256]{0,1:T(8,128)}), (f32[512,256]{0,1:T(8,128)}, f32[512,256]{0,1:T(8,128)})) %all-reduce.15.cloned.1.call-update) | async-done | bytes 1048592 | tf_op jit(solution)/shard_map/psum | solution.py:11
  1113.7 3.2 fusion.1
  1116.9 3.4 subtract_subtract_fusion
  (43 shorter events, 0.7 us)
Async XLA Ops:
  7.2 215.3 %all-reduce.9.cloned.1.call-start = ((), (), s32[]{:S(2)}) async-start(), calls=%async_computation | async-start | bytes 524288 | tf_op jit(solution)/shard_map/psum | solution.py:51
  10.1 490.6 %all-reduce.17.cloned.1.call-start = ((), (), s32[]{:S(2)}) async-start(), calls=%async_computation.4 | async-start | bytes 2621440 | tf_op jit(solution)/shard_map/psum | solution.py:11
  11.9 273.4 %copy-start.2 = (f32[512,256]{1,0:T(8,128)S(1)}, f32[512,256]{1,0:T(8,128)}, u32[]{:S(2)}) copy-start(f32[512,256]{1,0:T(8,128)} %param.5) | copy-start | bytes 1572868
  286.7 0.7 copy-start.1
  288.6 397.4 %all-reduce.11.cloned.1.call-start = ((), (), s32[]{:S(2)}) async-start(), calls=%async_computation.1 | async-start | bytes 1048576 | tf_op jit(solution)/shard_map/psum | solution.py:62
  540.9 27.8 %copy-start = (f32[512,1024]{1,0:T(8,128)S(1)}, f32[512,1024]{1,0:T(8,128)}, u32[]{:S(2)}) copy-start(f32[512,1024]{1,0:T(8,128)} %param.6) | copy-start | bytes 6291460
  545.1 21.4 %copy-start.5 = (f32[256,256]{1,0:T(8,128)}, f32[256,256]{1,0:T(8,128)S(1)}, u32[]{:S(2)}) copy-start(f32[256,256]{1,0:T(8,128)S(1)} %get-tuple-element.193) | copy-start | bytes 786436
  564.8 1.7 copy-start.7
  565.1 1.4 copy-start.6
  571.4 326.9 %all-reduce.13.cloned.1.call-start = ((), (), s32[]{:S(2)}) async-start(), calls=%async_computation.2 | async-start | bytes 524288 | tf_op jit(solution)/shard_map/psum | solution.py:64
  688.1 0.8 copy-start.3
  691.2 422.5 %all-reduce.15.cloned.1.call-start = ((), (), s32[]{:S(2)}) async-start(), calls=%async_computation.3 | async-start | bytes 2097152 | tf_op jit(solution)/shard_map/psum | solution.py:11
  1113.7 3.2 copy-start.4
Sparse Core Ops, SparseCore 0:
  10.9 211.5 all-reduce.8
  288.7 211.9 all-reduce.16
  571.6 114.3 all-reduce.10
  691.3 206.9 all-reduce.12
  902.9 210.7 all-reduce.14
where the time goes:
time: 1140 us; the launch traced here: 1130 us
  waiting for transfers between devices  947 us (83%)
  other arithmetic  113 us (10%)
  matrix products  32.8 us (3%)
  between operations  17 us (1%)
  local copies, waits for them, and re-layouts  16.8 us (1%)
    psum x2, waiting for transfers between devices, from_root(): return lax.psum(jnp.where(mine, value, jnp.zeros_like(value)), axis)  421 us
    psum x1, waiting for transfers between devices, body(): gram, top_panel = lax.psum((product_tn(panel, panel), top_panel), 'row')  211 us
    psum x1, waiting for transfers between devices, body(): paired = lax.psum(product_tn(reflect_rows, projected), 'row')  205 us
    psum x1, waiting for transfers between devices, body(): summed = lax.psum(product(trailing, reflect_cols), 'col')  110 us
    another operation x7, other arithmetic, reflector_inverse(): chol_factor = jnp.linalg.cholesky(normal_eq)  34.6 us
    another operation x6, other arithmetic, body(): factor = jnp.linalg.cholesky(gram)  34 us
  transfers between devices with their start and end apart: 5, of which 5 were waited for; matrix products, arithmetic and copies ran while one was open for 1% of the time, Pallas kernels for 0%

commit v1 on v0

v1 whole, which is shorter than its diff:
```python
import jax
import jax.numpy as jnp
from jax import lax
from jax.sharding import PartitionSpec as P

highest = lax.Precision.HIGHEST


def product(left, right):
    return jnp.dot(left, right, precision=highest, preferred_element_type=jnp.float32)


def product_nt(left, right):
    return lax.dot_general(
        left, right, (((1,), (1,)), ((), ())), precision=highest, preferred_element_type=jnp.float32
    )


def product_tn(left, right):
    return lax.dot_general(
        left, right, (((0,), (0,)), ((), ())), precision=highest, preferred_element_type=jnp.float32
    )


def pair_sum(value):
    rows = lax.axis_size("row")
    return value + lax.ppermute(value, "row", [(i, i ^ 1) for i in range(rows)])


def spread(value, axis, count, groups=None):
    copies = jnp.broadcast_to(value[None], (count, *value.shape))
    return lax.all_to_all(copies, axis, 0, 0, axis_index_groups=groups)


def chips_sum(value):
    chips = lax.axis_size("row") // 2
    groups = [[2 * z + k for z in range(chips)] for k in range(2)]
    return jnp.sum(spread(pair_sum(value), "row", chips, groups), axis=0)


def from_first(value):
    rows = lax.axis_size("row")
    value = jnp.where(lax.axis_index("row") == 0, value, jnp.zeros_like(value))
    step = rows // 2
    while step >= 1:
        pairs = [(i, i + step) for i in range(0, rows, 2 * step)]
        value = value + lax.ppermute(value, "row", pairs)
        step //= 2
    return value


def to_columns(piece):
    rows, cols = lax.axis_size("row"), lax.axis_size("col")
    pairs = []
    for z in range(rows // 2):
        for k in range(2):
            for c in range(cols):
                pairs.append(((2 * z + k) * cols + c, (2 * c + k) * cols + z))
    turned = lax.ppermute(piece, ("row", "col"), pairs)
    gathered = lax.all_gather(turned, "row", axis=0, tiled=False)
    gathered = gathered.reshape(rows // 2, 2, *piece.shape).transpose(1, 0, 2, 3)
    return gathered.reshape(rows * piece.shape[0], piece.shape[1])


def body(panel, trailing):
    row_count, width = panel.shape
    cols = lax.axis_size("col")
    row_index = lax.axis_index("row")
    col_index = lax.axis_index("col")
    piece_rows = row_count // cols
    part_rows = width // cols

    panel_piece = lax.dynamic_slice_in_dim(panel, col_index * piece_rows, piece_rows, 0)
    panel_cols = to_columns(panel_piece)
    top_panel = from_first(panel[:width])

    gram_here = product_tn(panel, panel)
    gram_part = lax.dynamic_slice_in_dim(gram_here, col_index * part_rows, part_rows, 0)
    gram = spread(chips_sum(gram_part), "col", cols).reshape(width, width)
    factor = jnp.linalg.cholesky(gram)
    band_block = -factor.T

    top_add = jnp.pad(factor.T, ((0, row_count - width), (0, 0)))
    vectors = panel + jnp.where(row_index == 0, top_add, 0.0)
    top_add = jnp.pad(factor.T, ((0, panel_cols.shape[0] - width), (0, 0)))
    vector_cols = panel_cols + jnp.where(col_index == 0, top_add, 0.0)

    partial = product(trailing, vector_cols)
    inner = product_tn(vectors, partial)
    sent = jnp.concatenate(
        [partial.reshape(cols, piece_rows, width), inner.reshape(cols, part_rows, width)], axis=1
    )
    mine = jnp.sum(lax.all_to_all(sent, "col", 0, 0), axis=0)
    image_piece = mine[:piece_rows]
    image_cols = to_columns(image_piece)
    inner_part = chips_sum(mine[piece_rows:])
    shared = spread(jnp.concatenate([image_piece, inner_part], axis=0), "col", cols)
    image = shared[:, :piece_rows].reshape(row_count, width)
    inner = shared[:, piece_rows:].reshape(width, width)

    identity = jnp.eye(width, dtype=jnp.float32)
    factor_inverse = jax.scipy.linalg.solve_triangular(factor, identity, lower=True)
    shifted = identity + product_nt(factor_inverse, top_panel)
    chol_factor = jnp.linalg.cholesky(product_tn(shifted, shifted))
    inverse_top = jax.scipy.linalg.cho_solve((chol_factor, True), shifted.T)
    middle = product(product_tn(factor_inverse, inverse_top.T), factor_inverse)
    half = 0.5 * product_tn(middle, product(inner, middle))
    correction = product(image, middle) - product(vectors, half)
    correction_cols = product(image_cols, middle) - product(vector_cols, half)
    updated = (
        trailing - product_nt(vectors, correction_cols) - product_nt(correction, vector_cols)
    )
    return (band_block, updated)


def solution(mesh):
    in_specs = (P("row", None), P("row", "col"))
    out_specs = (P(), P("row", "col"))
    return jax.shard_map(body, mesh=mesh, in_specs=in_specs, out_specs=out_specs, check_vma=False)
```

time: 1140 us -> 350 us (0.31)
  waiting for transfers between devices: 947 us -> 79.6 us
  starting transfers between devices: 0.42 us -> 90 us
    psum x5 -> x0, waiting for transfers between devices: 947 us -> none  [the longest x2 421 us: from_root(): return lax.psum(jnp.where(mine, value, jnp.zeros_like(value)), axis)]
    all_to_all x0 -> x5, starting transfers between devices: none -> 60.2 us  [the longest x4 52.5 us: spread(): return lax.all_to_all(copies, axis, 0, 0, axis_index_groups=groups)]
    all_gather x0 -> x2, waiting for transfers between devices: none -> 54.9 us  [to_columns(): gathered = lax.all_gather(turned, 'row', axis=0, tiled=False)]
    ppermute x0 -> x9, starting transfers between devices: none -> 29.7 us  [the longest x2 23.9 us: pair_sum(): return value + lax.ppermute(value, 'row', [(i, i ^ 1) for i in range(rows)])]
    all_to_all x0 -> x5, waiting for transfers between devices: none -> 24.7 us  [the longest x4 24.7 us: spread(): return lax.all_to_all(copies, axis, 0, 0, axis_index_groups=groups)]
  transfers between devices with their start and end apart: 5 -> 16, of which waited for: 5 -> 5; matrix products, arithmetic and copies ran while one was open for 1% -> 40% of each run, Pallas kernels for 0% -> 0%
where the time goes in v1:
time: 350 us; the launch traced here: 347 us
  other arithmetic  113 us (32%)
  starting transfers between devices  90 us (26%)
  waiting for transfers between devices  79.6 us (23%)
  matrix products  29 us (8%)
  between operations  17.5 us (5%)
  local copies, waits for them, and re-layouts  17.4 us (5%)
    all_gather x2, waiting for transfers between devices, to_columns(): gathered = lax.all_gather(turned, 'row', axis=0, tiled=False)  54.9 us
    all_to_all x4, starting transfers between devices, spread(): return lax.all_to_all(copies, axis, 0, 0, axis_index_groups=groups)  52.5 us
    another operation x7, other arithmetic, body(): chol_factor = jnp.linalg.cholesky(product_tn(shifted, shifted))  35.2 us
    another operation x6, other arithmetic, body(): factor = jnp.linalg.cholesky(gram)  33.9 us
    all_to_all x4, waiting for transfers between devices, spread(): return lax.all_to_all(copies, axis, 0, 0, axis_index_groups=groups)  24.7 us
    ppermute x2, starting transfers between devices, pair_sum(): return value + lax.ppermute(value, 'row', [(i, i ^ 1) for i in range(rows)])  23.9 us
    another operation x2, other arithmetic, body(): inverse_top = jax.scipy.linalg.cho_solve((chol_factor, True), shifted.T)  20.7 us
    another operation x3, other arithmetic, body(): jax.scipy.linalg.solve_triangular(factor, identity, lower=True)  19.9 us
  transfers between devices with their start and end apart: 16, of which 5 were waited for; matrix products, arithmetic and copies ran while one was open for 40% of the time, Pallas kernels for 0%

profile of v1, /device:TPU:1, one launch (start us, length us, event | category | flops | bytes accessed | tf_op | source)
XLA Modules:
  0.0 346.5 jit_solution(11789374617258666785)
XLA Ops:
  7.2 2.3 fusion.50
  9.5 8.8 %collective-permute-start = (f32[16,256]{1,0:T(8,128)S(1)}, f32[16,256]{1,0:T(8,128)S(1)}, u32[]{:S(2)}, u32[]{:S(2)}) collective-permute-start(f32[16,256]{1,0:T(8,128)S(1)} %constant_dynamic-slice_fusion.3), channel_id=1, source_target_pairs={{0,16},{16,0},{32,48},{48,32},{64,80},{80,64},{96,112},{112,96},{1... | collective-permute-start | bytes 49160 | tf_op jit(solution)/shard_map/ppermute | solution.py:27
  18.3 1.0 slice_select_fusion
  19.2 0.7 collective-permute-start.3
  20.0 0.7 broadcast_in_dim.19
  20.7 9.5 %all-to-all-start = ((f32[16,16,256]{2,1,0:T(8,128)}), f32[16,16,256]{2,1,0:T(8,128)S(1)}, u32[]{:S(2)}, u32[]{:S(2)}) async-start(f32[16,16,256]{2,1,0:T(8,128)} %broadcast_in_dim.19), calls=%async_computation | async-start | bytes 524288 | tf_op jit(solution)/shard_map/all_to_all | solution.py:32
  30.3 0.7 collective-permute-start.4
  31.0 0.7 collective-permute-start.5
  31.8 0.7 collective-permute-start.6
  32.5 10.1 %all-to-all-done = f32[16,16,256]{2,1,0:T(8,128)S(1)} async-done(((f32[16,16,256]{2,1,0:T(8,128)}), f32[16,16,256]{2,1,0:T(8,128)S(1)}, u32[]{:S(2)}, u32[]{:S(2)}) %all-to-all-start) | async-done | bytes 262176 | tf_op jit(solution)/shard_map/all_to_all | solution.py:32
  42.6 0.7 broadcast_in_dim.20
  43.3 6.8 %all-to-all-start.1 = ((f32[16,16,256]{2,1,0:T(8,128)}), f32[16,16,256]{2,1,0:T(8,128)S(1)}, u32[]{:S(2)}, u32[]{:S(2)}) async-start(f32[16,16,256]{2,1,0:T(8,128)} %broadcast_in_dim.20), calls=%async_computation.1 | async-start | bytes 524288 | tf_op jit(solution)/shard_map/all_to_all | solution.py:32
  50.1 0.7 collective-permute-start.1
  51.1 0.6 copy-done.5
  51.8 1.8 collective-permute-start.7
  53.5 4.1 %all-to-all-done.1 = f32[16,16,256]{2,1,0:T(8,128)S(1)} async-done(((f32[16,16,256]{2,1,0:T(8,128)}), f32[16,16,256]{2,1,0:T(8,128)S(1)}, u32[]{:S(2)}, u32[]{:S(2)}) %all-to-all-start.1) | async-done | bytes 262176 | tf_op jit(solution)/shard_map/all_to_all | solution.py:32
  57.8 11.7 %cholesky.130 = f32[128,128]{1,0:T(8,128)S(1)} custom-call(f32[128,128]{1,0:T(8,128)S(1)} %cholesky.194), custom_call_target="Cholesky" | custom-call | tf_op jit(solution)/shard_map/jit(cholesky)/cholesky | solution.py:80
  69.5 9.8 %custom-call.18 = f32[1,128,128]{1,2,0:T(8,128)S(1)} custom-call(f32[1,128,128]{2,1,0:T(8,128)S(1)} %get-tuple-element.65), custom_call_target="InvertDiagBlocksLowerTriangular" | custom-call | tf_op jit(solution)/shard_map/jit(cholesky)/cholesky | solution.py:80
  79.9 11.7 %cholesky.147 = f32[128,128]{1,0:T(8,128)S(1)} custom-call(f32[128,128]{1,0:T(8,128)S(1)} %convolution_subtract_fusion.5), custom_call_target="Cholesky" | custom-call | tf_op jit(solution)/shard_map/jit(cholesky)/cholesky | solution.py:80
  91.6 0.6 compare_reduce_fusion.2
  93.6 3.8 %while.6 = (s32[]{:T(128)}, f32[256,256]{1,0:T(8,128)S(1)}, s32[2,2]{1,0:T(2,128)S(1)}, f32[2,128,128]{2,1,0:T(8,128)S(1)}, s32[]{:T(128)}) while((s32[]{:T(128)}, f32[256,256]{1,0:T(8,128)S(1)}, s32[2,2]{1,0:T(2,128)S(1)}, f32[2,128,128]{2,1,0:T(8,128)S(1)}, s32[]{:T(128)}) %tuple.56), condition=%wide.while_cond, body=%wide.while_body.sunk | while | flops 2 | bytes 131189 | solution.py:102
  94.2 1.3 bitcast_dynamic-update-slice_fusion.5
  96.1 1.3 bitcast_dynamic-update-slice_fusion.5
  97.5 19.8 %custom-call.19 = f32[2,128,128]{1,2,0:T(8,128)S(1)} custom-call(f32[2,128,128]{2,1,0:T(8,128)S(1)} %get-tuple-element.26), custom_call_target="InvertDiagBlocksLowerTriangular" | custom-call | tf_op jit(solution)/shard_map/jit(_solve_triangular)/triangular_solve/custom-call.1 | solution.py:102
  117.9 0.8 copy.33
  120.3 11.7 %cholesky.164 = f32[128,128]{1,0:T(8,128)S(1)} custom-call(f32[128,128]{1,0:T(8,128)S(1)} %cholesky.197), custom_call_target="Cholesky" | custom-call | tf_op jit(solution)/shard_map/jit(cholesky)/cholesky | solution.py:104
  132.1 9.8 %custom-call.20 = f32[1,128,128]{1,2,0:T(8,128)S(1)} custom-call(f32[1,128,128]{2,1,0:T(8,128)S(1)} %get-tuple-element.61), custom_call_target="InvertDiagBlocksLowerTriangular" | custom-call | tf_op jit(solution)/shard_map/jit(cholesky)/cholesky | solution.py:104
  141.9 0.7 cholesky.189
  142.6 11.0 %all-gather.5.cloned.1.call-done = f32[1024,256]{1,0:T(8,128)} async-done(((f32[32,256]{1,0:T(8,128)}), f32[1024,256]{1,0:T(8,128)}) %all-gather.5.cloned.1.call-update) | async-done | bytes 1048592 | tf_op jit(solution)/shard_map/all_gather | solution.py:60
  153.7 1.3 copy.27
  155.3 3.5 %fusion.1 = f32[256,512]{1,0:T(8,128)S(1)} fusion(f32[512,1024]{1,0:T(8,128)} %param.6, f32[1024,256]{0,1:T(8,128)S(1)} %copy.28, f32[256,256]{0,1:T(8,128)S(1)} %get-tuple-element.53, pred[]{:T(512)S(6)} %eq.16), kind=kOutput, calls=%fused_computation.16 | convolution fusion | flops 1611137024 | bytes 3932161 | tf_op jit(solution)/shard_map/dot_general | solution.py:10
  158.9 1.3 fusion.23
  160.4 1.9 pad_maximum_fusion
  162.3 7.7 %all-to-all-start.2 = ((f32[16,48,256]{2,1,0:T(8,128)}), f32[16,48,256]{2,1,0:T(8,128)S(1)}, u32[]{:S(2)}, u32[]{:S(2)}) async-start(f32[16,48,256]{2,1,0:T(8,128)} %pad_maximum_fusion), calls=%async_computation.2 | async-start | bytes 1572864 | tf_op jit(solution)/shard_map/all_to_all | solution.py:93
  170.0 1.7 constant_dynamic-update-slice_fusion
  171.7 1.1 convolution_subtract_fusion.4
  172.8 11.7 %cholesky.181 = f32[128,128]{1,0:T(8,128)S(1)} custom-call(f32[128,128]{1,0:T(8,128)S(1)} %convolution_subtract_fusion.4), custom_call_target="Cholesky" | custom-call | tf_op jit(solution)/shard_map/jit(cholesky)/cholesky | solution.py:104
  184.5 0.7 compare_reduce_fusion.1
  185.2 0.6 select_reduce_fusion
  185.8 0.6 compare_reduce_fusion
  187.7 15.1 %collective-permute-start.8 = (f32[16,256]{1,0:T(8,128)S(1)}, f32[16,256]{1,0:T(8,128)S(1)}, u32[]{:S(2)}, u32[]{:S(2)}) collective-permute-start(f32[16,256]{1,0:T(8,128)S(1)} %slice.120), channel_id=1, source_target_pairs={{0,16},{16,0},{32,48},{48,32},{64,80},{80,64},{96,112},{112,96},{1... | collective-permute-start | bytes 49160 | tf_op jit(solution)/shard_map/ppermute | solution.py:27
  202.9 1.0 select_select_fusion
  203.9 0.7 broadcast_in_dim.41
  204.6 12.3 %all-to-all-start.3 = ((f32[16,16,256]{2,1,0:T(8,128)}), f32[16,16,256]{2,1,0:T(8,128)S(1)}, u32[]{:S(2)}, u32[]{:S(2)}) async-start(f32[16,16,256]{2,1,0:T(8,128)} %broadcast_in_dim.41), calls=%async_computation.3 | async-start | bytes 524288 | tf_op jit(solution)/shard_map/all_to_all | solution.py:32
  216.9 3.9 %while.5 = (s32[]{:T(128)}, f32[256,256]{1,0:T(8,128)S(1)}, s32[2,2]{1,0:T(2,128)S(1)}, f32[2,128,128]{2,1,0:T(8,128)S(1)}, s32[]{:T(128)}) while((s32[]{:T(128)}, f32[256,256]{1,0:T(8,128)S(1)}, s32[2,2]{1,0:T(2,128)S(1)}, f32[2,128,128]{2,1,0:T(8,128)S(1)}, s32[]{:T(128)}) %tuple.66), condition=%wide.while_cond.1, body=%wide.while_body.1.sunk | while | flops 2 | bytes 131189 | solution.py:105
  217.0 0.6 fusion.84
  217.6 1.3 bitcast_dynamic-update-slice_fusion.4
  218.9 0.6 fusion.84
  219.5 1.3 bitcast_dynamic-update-slice_fusion.4
  220.8 19.7 %custom-call.15 = f32[2,128,128]{1,2,0:T(8,128)S(1)} custom-call(f32[2,128,128]{2,1,0:T(8,128)S(1)} %get-tuple-element.19), custom_call_target="InvertDiagBlocksLowerTriangular" | custom-call | tf_op jit(solution)/shard_map/jit(_cho_solve)/triangular_solve | solution.py:105
  241.5 0.7 collective-permute-start.2
  242.5 0.6 copy-done.6
  243.2 1.0 broadcast_in_dim.42
  244.1 24.0 %all-to-all-start.4 = ((f32[16,48,256]{2,1,0:T(8,128)}), f32[16,48,256]{2,1,0:T(8,128)S(1)}, u32[]{:S(2)}, u32[]{:S(2)}) async-start(f32[16,48,256]{2,1,0:T(8,128)} %broadcast_in_dim.42), calls=%async_computation.4 | async-start | bytes 1572864 | tf_op jit(solution)/shard_map/all_to_all | solution.py:32
  268.4 1.1 fusion.32
  270.5 10.5 %all-to-all-done.4 = f32[16,48,256]{2,1,0:T(8,128)S(1)} async-done(((f32[16,48,256]{2,1,0:T(8,128)}), f32[16,48,256]{2,1,0:T(8,128)S(1)}, u32[]{:S(2)}, u32[]{:S(2)}) %all-to-all-start.4) | async-done | bytes 786464 | tf_op jit(solution)/shard_map/all_to_all | solution.py:32
  281.5 0.6 convolution_multiply_fusion
  282.7 1.8 convolution_subtract_fusion.1
  284.5 1.8 fusion
  286.3 43.8 %all-gather.7.cloned.1.call-done = f32[1024,256]{1,0:T(8,128)} async-done(((f32[32,256]{1,0:T(8,128)}), f32[1024,256]{1,0:T(8,128)}) %all-gather.7.cloned.1.call-update) | async-done | bytes 1048592 | tf_op jit(solution)/shard_map/all_gather | solution.py:60
  330.1 1.3 copy.30
  331.4 1.0 convolution_subtract_fusion
  332.5 3.5 %fusion.22 = f32[512,1024]{1,0:T(8,128)S(1)} fusion(f32[1024,256]{1,0:T(8,128)S(1)} %convolution_subtract_fusion, f32[512,256]{0,1:T(8,128)S(1)} %copy.26, f32[256,256]{0,1:T(8,128)S(1)} %get-tuple-element.53, pred[]{:T(512)S(6)} %eq.15), kind=kOutput, calls=%fused_computation.47 | convolution fusion | flops 1610874880 | bytes 3932161 | tf_op jit(solution)/shard_map/dot_general | solution.py:14
  336.0 3.4 subtract_subtract_fusion
  (85 shorter events, 9.0 us)
Async XLA Ops:
  7.2 23.1 %copy-start = (f32[512,256]{1,0:T(8,128)S(1)}, f32[512,256]{1,0:T(8,128)}, u32[]{:S(2)}) copy-start(f32[512,256]{1,0:T(8,128)} %param.5) | copy-start | bytes 1572868
  9.5 10.5 %collective-permute-start = (f32[16,256]{1,0:T(8,128)S(1)}, f32[16,256]{1,0:T(8,128)S(1)}, u32[]{:S(2)}, u32[]{:S(2)}) collective-permute-start(f32[16,256]{1,0:T(8,128)S(1)} %constant_dynamic-slice_fusion.3), channel_id=1, source_target_pairs={{0,16},{16,0},{32,48},{48,32},{64,80},{80,64},{96,112},{112,96},{1... | collective-permute-start | bytes 49160 | tf_op jit(solution)/shard_map/ppermute | solution.py:27
  19.2 11.0 %collective-permute-start.3 = (f32[256,256]{1,0:T(8,128)S(1)}, f32[256,256]{1,0:T(8,128)S(1)}, u32[]{:S(2)}, u32[]{:S(2)}) collective-permute-start(f32[256,256]{1,0:T(8,128)S(1)} %slice_select_fusion), channel_id=1, source_target_pairs={{0,256},{1,257},{2,258},{3,259},{4,260},{5,261},{6,262},{7,263},{8... | collective-permute-start | bytes 786440 | tf_op jit(solution)/shard_map/ppermute | solution.py:47
  20.7 21.9 %all-to-all-start = ((f32[16,16,256]{2,1,0:T(8,128)}), f32[16,16,256]{2,1,0:T(8,128)S(1)}, u32[]{:S(2)}, u32[]{:S(2)}) async-start(f32[16,16,256]{2,1,0:T(8,128)} %broadcast_in_dim.19), calls=%async_computation | async-start | bytes 524288 | tf_op jit(solution)/shard_map/all_to_all | solution.py:32
  30.3 0.7 collective-permute-start.4
  31.0 0.7 collective-permute-start.5
  31.8 19.9 %collective-permute-start.6 = (f32[256,256]{1,0:T(8,128)S(1)}, f32[256,256]{1,0:T(8,128)S(1)}, u32[]{:S(2)}, u32[]{:S(2)}) collective-permute-start(f32[256,256]{1,0:T(8,128)S(1)} %add.70), channel_id=1, source_target_pairs={{0,32},{64,96},{128,160},{192,224},{256,288},{320,352},{384,416},{... | collective-permute-start | bytes 786440 | tf_op jit(solution)/shard_map/ppermute | solution.py:47
  43.3 14.3 %all-to-all-start.1 = ((f32[16,16,256]{2,1,0:T(8,128)}), f32[16,16,256]{2,1,0:T(8,128)S(1)}, u32[]{:S(2)}, u32[]{:S(2)}) async-start(f32[16,16,256]{2,1,0:T(8,128)} %broadcast_in_dim.20), calls=%async_computation.1 | async-start | bytes 524288 | tf_op jit(solution)/shard_map/all_to_all | solution.py:32
  50.1 103.6 %all-gather.5.cloned.1.call-start = ((), (), s32[]{:S(2)}) async-start(), calls=%async_computation.5 | async-start | bytes 1081344 | tf_op jit(solution)/shard_map/all_gather | solution.py:60
  50.1 0.9 collective-permute-start.1
  51.1 0.6 copy-start.5
  51.8 67.3 %collective-permute-start.7 = (f32[256,256]{1,0:T(8,128)S(1)}, f32[256,256]{1,0:T(8,128)S(1)}, u32[]{:S(2)}, u32[]{:S(2)}) collective-permute-start(f32[256,256]{1,0:T(8,128)S(1)} %add.71), channel_id=1, source_target_pairs={{0,16},{32,48},{64,80},{96,112},{128,144},{160,176},{192,208},{224... | collective-permute-start | bytes 786440 | tf_op jit(solution)/shard_map/ppermute | solution.py:47
  120.3 34.7 %copy-start.3 = (f32[256,256]{1,0:T(8,128)}, f32[256,256]{1,0:T(8,128)S(1)}, u32[]{:S(2)}) copy-start(f32[256,256]{1,0:T(8,128)S(1)} %fusion.6) | copy-start | bytes 786436
  162.3 25.4 %all-to-all-start.2 = ((f32[16,48,256]{2,1,0:T(8,128)}), f32[16,48,256]{2,1,0:T(8,128)S(1)}, u32[]{:S(2)}, u32[]{:S(2)}) async-start(f32[16,48,256]{2,1,0:T(8,128)} %pad_maximum_fusion), calls=%async_computation.2 | async-start | bytes 1572864 | tf_op jit(solution)/shard_map/all_to_all | solution.py:93
  187.7 16.1 %collective-permute-start.8 = (f32[16,256]{1,0:T(8,128)S(1)}, f32[16,256]{1,0:T(8,128)S(1)}, u32[]{:S(2)}, u32[]{:S(2)}) collective-permute-start(f32[16,256]{1,0:T(8,128)S(1)} %slice.120), channel_id=1, source_target_pairs={{0,16},{16,0},{32,48},{48,32},{64,80},{80,64},{96,112},{112,96},{1... | collective-permute-start | bytes 49160 | tf_op jit(solution)/shard_map/ppermute | solution.py:27
  204.6 38.5 %all-to-all-start.3 = ((f32[16,16,256]{2,1,0:T(8,128)}), f32[16,16,256]{2,1,0:T(8,128)S(1)}, u32[]{:S(2)}, u32[]{:S(2)}) async-start(f32[16,16,256]{2,1,0:T(8,128)} %broadcast_in_dim.41), calls=%async_computation.3 | async-start | bytes 524288 | tf_op jit(solution)/shard_map/all_to_all | solution.py:32
  216.9 113.2 %all-gather.7.cloned.1.call-start = ((), (), s32[]{:S(2)}) async-start(), calls=%async_computation.6 | async-start | bytes 1081344 | tf_op jit(solution)/shard_map/all_gather | solution.py:60
  240.5 3.7 %copy-start.4 = (f32[2,128,128]{1,2,0:T(8,128)}, f32[2,128,128]{1,2,0:T(8,128)S(1)}, u32[]{:S(2)}) copy-start(f32[2,128,128]{1,2,0:T(8,128)S(1)} %custom-call.15) | copy-start | bytes 393220
  241.5 0.9 collective-permute-start.2
  242.5 0.6 copy-start.6
  244.1 36.9 %all-to-all-start.4 = ((f32[16,48,256]{2,1,0:T(8,128)}), f32[16,48,256]{2,1,0:T(8,128)S(1)}, u32[]{:S(2)}, u32[]{:S(2)}) async-start(f32[16,48,256]{2,1,0:T(8,128)} %broadcast_in_dim.42), calls=%async_computation.4 | async-start | bytes 1572864 | tf_op jit(solution)/shard_map/all_to_all | solution.py:32
  332.4 3.5 %copy-start.1 = (f32[512,1024]{1,0:T(8,128)S(1)}, f32[512,1024]{1,0:T(8,128)}, u32[]{:S(2)}) copy-start(f32[512,1024]{1,0:T(8,128)} %param.6) | copy-start | bytes 6291460
  332.5 3.5 %copy-start.2 = (f32[512,256]{1,0:T(8,128)S(1)}, f32[512,256]{1,0:T(8,128)}, u32[]{:S(2)}) copy-start(f32[512,256]{1,0:T(8,128)} %convolution_subtract_fusion.1) | copy-start | bytes 1572868
Sparse Core Ops, SparseCore 0:
  53.6 100.0 all-gather.4
  243.3 86.8 all-gather.6

commit v2 on v1

v2 whole, which is shorter than its diff:
```python
import functools

import jax
import jax.numpy as jnp
from jax import lax
from jax.experimental import pallas as pl
from jax.experimental.pallas import tpu as pltpu
from jax.sharding import PartitionSpec as P

highest = lax.Precision.HIGHEST


def product(left, right):
    return jnp.dot(left, right, precision=highest, preferred_element_type=jnp.float32)


def product_nt(left, right):
    return lax.dot_general(
        left, right, (((1,), (1,)), ((), ())), precision=highest, preferred_element_type=jnp.float32
    )


def product_tn(left, right):
    return lax.dot_general(
        left, right, (((0,), (0,)), ((), ())), precision=highest, preferred_element_type=jnp.float32
    )


def swapped(value):
    return lax.ppermute(value, "row", [(i, i ^ 1) for i in range(lax.axis_size("row"))])


def both_cores(value):
    other = swapped(value)
    first = lax.axis_index("row") % 2 == 0
    return jnp.where(first, value, other), jnp.where(first, other, value)


def spread(value, axis, groups=None):
    count = lax.axis_size(axis) if groups is None else len(groups[0])
    copies = jnp.broadcast_to(value[None], (count, *value.shape))
    return lax.all_to_all(copies, axis, 0, 0, axis_index_groups=groups)


def spread_chips(value):
    chips = lax.axis_size("row") // 2
    return spread(value, "row", [[2 * z + k for z in range(chips)] for k in range(2)])


def turn(piece):
    rows, cols = lax.axis_size("row"), lax.axis_size("col")
    pairs = []
    for z in range(rows // 2):
        for k in range(2):
            for c in range(cols):
                pairs.append(((2 * z + k) * cols + c, (2 * c + k) * cols + z))
    return lax.ppermute(piece, ("row", "col"), pairs)


def factor_kernel(gram_ref, top_ref, upper_ref, middle_ref, left, right, *, block):
    width = gram_ref.shape[0]
    rows = lax.broadcasted_iota(jnp.int32, (width, width), 0)
    cols = lax.broadcasted_iota(jnp.int32, (width, width), 1)
    left[:, :width] = gram_ref[...]
    left[:, width:] = jnp.where(rows == cols, 1.0, 0.0)
    right[:, :width] = top_ref[...]
    right[:, width:] = jnp.zeros((width, width), jnp.float32)
    inside = lax.broadcasted_iota(jnp.int32, (block, 1), 0)
    wide_row = lax.broadcasted_iota(jnp.int32, (block, 2 * width), 0)
    wide_col = lax.broadcasted_iota(jnp.int32, (block, 2 * width), 1)
    all_rows = lax.broadcasted_iota(jnp.int32, (width, block), 0)
    for start in range(0, width, block):
        stop = start + block
        part = left[start:stop, :]
        for j in range(block):
            column = part[:, start + j : start + j + 1]
            pivot = column[j : j + 1]
            scale = lax.rsqrt(pivot)
            scale = scale * (1.5 - 0.5 * pivot * scale * scale)
            row = part[j : j + 1, :] * scale
            part = jnp.where(inside == j, row, part - jnp.where(inside > j, column * scale, 0.0) * row)
        part = jnp.where(wide_col >= wide_row + start, part, 0.0)
        upper_ref[start:stop, :] = part[:, :width]
        if stop < width:
            left[stop:, :] = left[stop:, :] - product_tn(part[:, stop:width], part)
        side = right[start:stop, :] + part
        for j in range(block):
            column = side[:, start + j : start + j + 1]
            row = side[j : j + 1, :] / column[j : j + 1]
            side = jnp.where(inside == j, row, side - column * row)
        others = jnp.where((all_rows < start) | (all_rows >= stop), right[:, start:stop], 0.0)
        right[...] = right[...] - product(others, side)
        right[start:stop, :] = side
    middle_ref[...] = right[:, width:]

def factor(gram, top, block=32):
    width=gram.shape[0]
    sq=jax.ShapeDtypeStruct((width,width),jnp.float32)
    return pl.pallas_call(functools.partial(factor_kernel,block=block), out_shape=(sq,sq),
        scratch_shapes=[pltpu.VMEM((width,2*width),jnp.float32)]*2)(gram, top)


def body(panel, trailing):
    row_count, width = panel.shape
    rows, cols = lax.axis_size("row"), lax.axis_size("col")
    row_index = lax.axis_index("row")
    col_index = lax.axis_index("col")
    core = row_index % 2
    piece_rows = row_count // cols
    part_rows = width // cols
    half_rows = part_rows // 2

    def cut(value, start, size):
        return lax.dynamic_slice_in_dim(value, start, size, 0)

    turned = turn(cut(panel, col_index * piece_rows, piece_rows))
    gram_here = product_tn(panel, panel)
    mine = col_index * part_rows + core * half_rows
    theirs = col_index * part_rows + (1 - core) * half_rows
    received = swapped(
        jnp.concatenate([cut(gram_here, theirs, half_rows), cut(panel, theirs, half_rows)], axis=0)
    )
    gram_half = cut(gram_here, mine, half_rows) + received[:half_rows]
    top_half = jnp.where(core == 0, cut(panel, mine, half_rows), received[half_rows:])
    halves = jnp.concatenate([gram_half, top_half], axis=0)
    halves, turned = lax.optimization_barrier((halves, turned))
    gathered = lax.all_gather(turned, "row", axis=0, tiled=False)
    stacked = spread_chips(halves)
    halves = jnp.concatenate([jnp.sum(stacked[:, :half_rows], axis=0), stacked[0, half_rows:]], axis=0)
    pair = jnp.stack(both_cores(spread(halves, "col")), axis=1)
    gram = pair[:, :, :half_rows].reshape(width, width)
    top_panel = pair[:, :, half_rows:].reshape(width, width)
    upper, middle = factor(gram, top_panel)
    band_block = -upper

    panel_cols = gathered.reshape(rows // 2, 2, piece_rows, width).transpose(1, 0, 2, 3)
    panel_cols = panel_cols.reshape(rows * piece_rows, width)
    top_add = jnp.pad(upper, ((0, row_count - width), (0, 0)))
    vectors = panel + jnp.where(row_index == 0, top_add, 0.0)
    top_add = jnp.pad(upper, ((0, panel_cols.shape[0] - width), (0, 0)))
    vector_cols = panel_cols + jnp.where(col_index == 0, top_add, 0.0)

    partial = product(trailing, vector_cols)
    inner = product_tn(vectors, partial)
    sent = jnp.concatenate(
        [partial.reshape(cols, piece_rows, width), inner.reshape(cols, part_rows, width)], axis=1
    )
    summed = jnp.sum(lax.all_to_all(sent, "col", 0, 0), axis=0)
    image_piece = summed[:piece_rows]
    inner_part = summed[piece_rows:]
    image_turned = turn(image_piece)
    inner_part = jnp.sum(spread_chips(inner_part + swapped(inner_part)), axis=0)
    shared = spread(jnp.concatenate([image_piece, inner_part], axis=0), "col")
    image = shared[:, :piece_rows].reshape(row_count, width)
    inner = shared[:, piece_rows:].reshape(width, width)
    image_cols = spread_chips(image_turned).reshape(row_count, width)
    image_cols = jnp.concatenate(both_cores(image_cols), axis=0)

    half = 0.5 * product_tn(middle, product(inner, middle))
    correction = product(image, middle) - product(vectors, half)
    correction_cols = product(image_cols, middle) - product(vector_cols, half)
    updated = (
        trailing - product_nt(vectors, correction_cols) - product_nt(correction, vector_cols)
    )
    return (band_block, updated)


def solution(mesh):
    in_specs = (P("row", None), P("row", "col"))
    out_specs = (P(), P("row", "col"))
    return jax.shard_map(body, mesh=mesh, in_specs=in_specs, out_specs=out_specs, check_vma=False)
```

time: 350 us -> 254 us (0.73)
  other arithmetic: 113 us -> 2.62 us
  blocking collectives: 0 us -> 33.9 us
  Pallas kernels: 0 us -> 33.2 us
  waiting for transfers between devices: 79.6 us -> 61.3 us
  matrix products: 29 us -> 16.2 us
  local copies, waits for them, and re-layouts: 17.4 us -> 6.83 us
  starting transfers between devices: 90 us -> 84.2 us
    another operation x18 -> x2, other arithmetic: 110 us -> 0.86 us  [body(): pair = jnp.stack(both_cores(spread(halves, 'col')), axis=1)]
    all_gather x2 -> x1, waiting for transfers between devices: 54.9 us -> 3.75 us  [body(): gathered = lax.all_gather(turned, 'row', axis=0, tiled=False)]
    all_to_all x0 -> x2, blocking collectives: none -> 33.9 us  [the longest x1 20.3 us: body(): summed = jnp.sum(lax.all_to_all(sent, 'col', 0, 0), axis=0)]
    pallas_call x0 -> x1, Pallas kernels: none -> 33.2 us  [factor(): pl.pallas_call(functools.partial(factor_kernel, block=block), out_shape=(...]
    all_to_all x4, waiting for transfers between devices: 24.7 us -> 54.9 us  [spread(): return lax.all_to_all(copies, axis, 0, 0, axis_index_groups=groups)]
    another operation x19 -> x0, local copies, waits for them, and re-layouts: 8.44 us -> none  [the longest x9 3.88 us: body(): jax.scipy.linalg.solve_triangular(factor, identity, lower=True)]
    all_to_all x1 -> x0, starting transfers between devices: 7.72 us -> none  [body(): mine = jnp.sum(lax.all_to_all(sent, 'col', 0, 0), axis=0)]
    another operation x13 -> x0, matrix products: 6.81 us -> none  [the longest x2 2.78 us: body(): chol_factor = jnp.linalg.cholesky(product_tn(shifted, shifted))]
  transfers between devices with their start and end apart: 16 -> 11, of which waited for: 5 -> 7; matrix products, arithmetic and copies ran while one was open for 40% -> 2% of each run, Pallas kernels for 0% -> 13%
where the time goes in v2:
time: 254 us; the launch traced here: 253 us
  starting transfers between devices  84.2 us (33%)
  waiting for transfers between devices  61.3 us (24%)
  blocking collectives  33.9 us (13%)
  Pallas kernels  33.2 us (13%)
  matrix products  16.2 us (6%)
  between operations  14.4 us (6%)
  local copies, waits for them, and re-layouts  6.83 us (3%)
  other arithmetic  2.62 us (1%)
    all_to_all x4, waiting for transfers between devices, spread(): return lax.all_to_all(copies, axis, 0, 0, axis_index_groups=groups)  54.9 us
    all_to_all x4, starting transfers between devices, spread(): return lax.all_to_all(copies, axis, 0, 0, axis_index_groups=groups)  51.1 us
    pallas_call x1, Pallas kernels, factor(): pl.pallas_call(functools.partial(factor_kernel, block=block), out_shape=(...  33.2 us
    ppermute x4, starting transfers between devices, swapped(): lax.ppermute(value, 'row', [(i, i ^ 1) for i in range(lax.axis_size('row'...  31.6 us
    all_to_all x1, blocking collectives, body(): summed = jnp.sum(lax.all_to_all(sent, 'col', 0, 0), axis=0)  20.3 us
    all_to_all x1, blocking collectives, spread(): return lax.all_to_all(copies, axis, 0, 0, axis_index_groups=groups)  13.7 us
    dot_general x6, matrix products, product(): jnp.dot(left, right, precision=highest, preferred_element_type=jnp.float32)  7.08 us
    dot_general x2, matrix products, product_nt(): lax.dot_general(left, right, (((1,), (1,)), ((), ())), precision=highest,...  5.32 us
  transfers between devices with their start and end apart: 11, of which 7 were waited for; matrix products, arithmetic and copies ran while one was open for 2% of the time, Pallas kernels for 13%

profile of v2, /device:TPU:1, one launch (start us, length us, event | category | flops | bytes accessed | tf_op | source)
XLA Modules:
  0.0 252.6 jit_solution(8093556094220683519)
XLA Ops:
  7.2 2.2 fusion.10
  9.4 0.7 constant_dynamic-slice_fusion.1
  10.1 8.8 %collective-permute-start = (f32[16,256]{1,0:T(8,128)S(1)}, f32[16,256]{1,0:T(8,128)S(1)}, u32[]{:S(2)}, u32[]{:S(2)}) collective-permute-start(f32[16,256]{1,0:T(8,128)S(1)} %pad_maximum_fusion.3), channel_id=1, source_target_pairs={{0,16},{16,0},{32,48},{48,32},{64,80},{80,64},{96,112},{112,96},{1... | collective-permute-start | bytes 49160 | tf_op jit(solution)/shard_map/ppermute | solution.py:30
  18.9 0.8 constant_dynamic-slice_fusion
  19.7 0.7 collective-permute-start.1
  20.3 0.0 collective-permute-done
  20.4 0.7 slice_add_fusion
  21.1 0.0 collective-permute-done.1
  21.1 0.0 copy-start.5
  21.1 0.7 broadcast_in_dim.18
  21.8 24.0 %all-to-all-start = ((f32[16,16,256]{2,1,0:T(8,128)}), f32[16,16,256]{2,1,0:T(8,128)S(1)}, u32[]{:S(2)}, u32[]{:S(2)}) async-start(f32[16,16,256]{2,1,0:T(8,128)} %broadcast_in_dim.18), calls=%async_computation | async-start | bytes 524288 | tf_op jit(solution)/shard_map/all_to_all | solution.py:42
  45.9 0.0 all-gather.3.cloned.1.call-start
  45.9 0.0 copy-done.5
  45.9 0.7 all-gather.3.cloned.1.call-update
  46.6 12.0 %all-to-all-done = f32[16,16,256]{2,1,0:T(8,128)S(1)} async-done(((f32[16,16,256]{2,1,0:T(8,128)}), f32[16,16,256]{2,1,0:T(8,128)S(1)}, u32[]{:S(2)}, u32[]{:S(2)}) %all-to-all-start) | async-done | bytes 262176 | tf_op jit(solution)/shard_map/all_to_all | solution.py:42
  58.7 13.7 %all_to_all.30 = f32[16,16,256]{2,1,0:T(8,128)S(1)} all-to-all(f32[16,16,256]{2,1,0:T(8,128)S(1)} %broadcast_in_dim.19), channel_id=1, replica_groups=mesh['row'=32,'col'=16] {'col'}, dimensions={0} | all-to-all | bytes 524288 | tf_op jit(solution)/shard_map/all_to_all | solution.py:42
  72.4 9.7 %collective-permute-start.2 = (f32[16,16,256]{2,1,0:T(8,128)S(1)}, f32[16,16,256]{2,1,0:T(8,128)S(1)}, u32[]{:S(2)}, u32[]{:S(2)}) collective-permute-start(f32[16,16,256]{2,1,0:T(8,128)S(1)} %all_to_all.30), channel_id=1, source_target_pairs={{0,16},{16,0},{32,48},{48,32},{64,80},{80,64},{96,112},{112,96},{1... | collective-permute-start | bytes 786440 | tf_op jit(solution)/shard_map/ppermute | solution.py:30
  82.0 1.1 collective-permute-done.2
  83.2 0.8 pad_maximum_fusion.1
  84.0 33.2 %shard_map.41 = (f32[256,256]{1,0:T(8,128)}, f32[256,256]{1,0:T(8,128)}) custom-call(f32[256,256]{1,0:T(8,128)} %bitcast.48, f32[256,256]{1,0:T(8,128)} %bitcast.47), custom_call_target="tpu_custom_call" | custom-call | tf_op jit(solution)/shard_map/pallas_call | solution.py:99
  117.2 0.0 copy-start.3
  117.2 3.7 %all-gather.3.cloned.1.call-done = f32[1024,256]{1,0:T(8,128)} async-done(((f32[32,256]{1,0:T(8,128)}), f32[1024,256]{1,0:T(8,128)}) %all-gather.3.cloned.1.call-update) | async-done | bytes 1048592 | tf_op jit(solution)/shard_map/all_gather | solution.py:127
  121.0 0.0 copy-start.1
  121.0 1.5 copy.11
  122.4 0.0 copy-done.3
  122.5 0.1 bitcast_add_fusion
  122.5 0.3 copy-done.1
  122.9 0.0 copy-start
  122.9 3.6 %fusion.11 = f32[256,512]{1,0:T(8,128)S(1)} fusion(f32[1024,256]{1,0:T(8,128)S(1)} %bitcast_add_fusion, f32[512,1024]{1,0:T(8,128)S(1)} %copy-done.1), kind=kOutput, calls=%fused_computation.37 | convolution fusion | flops 1610612736 | bytes 3670016 | tf_op jit(solution)/shard_map/dot_general | solution.py:14
  126.4 0.2 copy.12
  126.6 0.0 copy-done
  126.6 1.0 fusion.5
  127.7 0.1 pad_maximum_fusion
  127.7 20.3 %all_to_all.31 = f32[16,48,256]{2,1,0:T(8,128)S(1)} all-to-all(f32[16,48,256]{2,1,0:T(8,128)S(1)} %pad_maximum_fusion), channel_id=1, replica_groups=mesh['row'=32,'col'=16] {'col'}, dimensions={0} | all-to-all | bytes 1572864 | tf_op jit(solution)/shard_map/all_to_all | solution.py:148
  148.0 0.1 reduce_sum.28
  148.1 3.3 %collective-permute-start.5 = (f32[16,256]{1,0:T(8,128)S(1)}, f32[16,256]{1,0:T(8,128)S(1)}, u32[]{:S(2)}, u32[]{:S(2)}) collective-permute-start(f32[16,256]{1,0:T(8,128)S(1)} %slice.47), channel_id=1, source_target_pairs={{0,16},{16,0},{32,48},{48,32},{64,80},{80,64},{96,112},{112,96},{1... | collective-permute-start | bytes 49160 | tf_op jit(solution)/shard_map/ppermute | solution.py:30
  151.4 0.8 collective-permute-done.5
  152.2 0.7 broadcast_in_dim.23
  152.9 7.8 %all-to-all-start.4 = ((f32[16,16,256]{2,1,0:T(8,128)}), f32[16,16,256]{2,1,0:T(8,128)S(1)}, u32[]{:S(2)}, u32[]{:S(2)}) async-start(f32[16,16,256]{2,1,0:T(8,128)} %broadcast_in_dim.23), calls=%async_computation.4 | async-start | bytes 524288 | tf_op jit(solution)/shard_map/all_to_all | solution.py:42
  160.8 14.0 %all-to-all-done.4 = f32[16,16,256]{2,1,0:T(8,128)S(1)} async-done(((f32[16,16,256]{2,1,0:T(8,128)}), f32[16,16,256]{2,1,0:T(8,128)S(1)}, u32[]{:S(2)}, u32[]{:S(2)}) %all-to-all-start.4) | async-done | bytes 262176 | tf_op jit(solution)/shard_map/all_to_all | solution.py:42
  174.8 1.0 broadcast_in_dim.44
  175.8 3.6 %all-to-all-start.5 = ((f32[16,48,256]{2,1,0:T(8,128)}), f32[16,48,256]{2,1,0:T(8,128)S(1)}, u32[]{:S(2)}, u32[]{:S(2)}) async-start(f32[16,48,256]{2,1,0:T(8,128)} %broadcast_in_dim.44), calls=%async_computation.5 | async-start | bytes 1572864 | tf_op jit(solution)/shard_map/all_to_all | solution.py:42
  179.4 0.0 copy-start.4
  179.4 0.8 collective-permute-start.3
  180.2 0.0 collective-permute-done.3
  180.2 9.7 %all-to-all-done.5 = f32[16,48,256]{2,1,0:T(8,128)S(1)} async-done(((f32[16,48,256]{2,1,0:T(8,128)}), f32[16,48,256]{2,1,0:T(8,128)S(1)}, u32[]{:S(2)}, u32[]{:S(2)}) %all-to-all-start.5) | async-done | bytes 786464 | tf_op jit(solution)/shard_map/all_to_all | solution.py:42
  189.9 0.8 broadcast_in_dim.22
  190.8 15.6 %all-to-all-start.3 = ((f32[16,32,256]{2,1,0:T(8,128)}), f32[16,32,256]{2,1,0:T(8,128)S(1)}, u32[]{:S(2)}, u32[]{:S(2)}) async-start(f32[16,32,256]{2,1,0:T(8,128)} %broadcast_in_dim.22), calls=%async_computation.3 | async-start | bytes 1048576 | tf_op jit(solution)/shard_map/all_to_all | solution.py:42
  206.4 0.7 neg.3
  207.2 0.0 copy-done.4
  207.2 0.4 fusion.12
  207.6 0.6 convolution_multiply_fusion
  208.2 0.6 fusion.14
  208.8 19.1 %all-to-all-done.3 = f32[16,32,256]{2,1,0:T(8,128)S(1)} async-done(((f32[16,32,256]{2,1,0:T(8,128)}), f32[16,32,256]{2,1,0:T(8,128)S(1)}, u32[]{:S(2)}, u32[]{:S(2)}) %all-to-all-start.3) | async-done | bytes 524320 | tf_op jit(solution)/shard_map/all_to_all | solution.py:42
  227.9 9.9 %collective-permute-start.4 = (f32[512,256]{1,0:T(8,128)S(1)}, f32[512,256]{1,0:T(8,128)S(1)}, u32[]{:S(2)}, u32[]{:S(2)}) collective-permute-start(f32[512,256]{1,0:T(8,128)S(1)} %bitcast.42), channel_id=1, source_target_pairs={{0,16},{16,0},{32,48},{48,32},{64,80},{80,64},{96,112},{112,96},{1... | collective-permute-start | bytes 1572872 | tf_op jit(solution)/shard_map/ppermute | solution.py:30
  237.8 0.6 convolution_subtract_fusion.1
  238.4 1.0 fusion.13
  239.4 0.0 collective-permute-done.4
  239.4 0.1 broadcast_select_fusion.1
  239.5 1.0 convolution_subtract_fusion
  240.4 0.0 copy-start.2
  240.5 1.9 fusion.4
  242.3 0.0 copy-done.2
  242.3 3.5 %subtract_subtract_fusion = f32[512,1024]{1,0:T(8,128)} fusion(f32[512,1024]{1,0:T(8,128)S(1)} %copy-done.2, f32[512,1024]{1,0:T(8,128)S(1)} %fusion.4, f32[512,256]{1,0:T(8,128)S(1)} %convolution_subtract_fusion.1, f32[1024,256]{1,0:T(8,128)S(1)} %bitcast_add_fusion), kind=kOutput, calls=%fused_computation | convolution fusion | flops 1611661312 | bytes 7864320 | tf_op jit(solution)/shard_map/dot_general | solution.py:18
  (14 shorter events, 0.2 us)
Async XLA Ops:
  10.1 10.2 %collective-permute-start = (f32[16,256]{1,0:T(8,128)S(1)}, f32[16,256]{1,0:T(8,128)S(1)}, u32[]{:S(2)}, u32[]{:S(2)}) collective-permute-start(f32[16,256]{1,0:T(8,128)S(1)} %pad_maximum_fusion.3), channel_id=1, source_target_pairs={{0,16},{16,0},{32,48},{48,32},{64,80},{80,64},{96,112},{112,96},{1... | collective-permute-start | bytes 49160 | tf_op jit(solution)/shard_map/ppermute | solution.py:30
  19.7 1.4 collective-permute-start.1
  21.1 24.8 %copy-start.5 = (f32[32,256]{1,0:T(8,128)}, f32[32,256]{1,0:T(8,128)S(1)}, u32[]{:S(2)}) copy-start(f32[32,256]{1,0:T(8,128)S(1)} %collective-permute-done.1) | copy-start | bytes 98308
  21.8 36.8 %all-to-all-start = ((f32[16,16,256]{2,1,0:T(8,128)}), f32[16,16,256]{2,1,0:T(8,128)S(1)}, u32[]{:S(2)}, u32[]{:S(2)}) async-start(f32[16,16,256]{2,1,0:T(8,128)} %broadcast_in_dim.18), calls=%async_computation | async-start | bytes 524288 | tf_op jit(solution)/shard_map/all_to_all | solution.py:42
  45.9 75.1 %all-gather.3.cloned.1.call-start = ((), (), s32[]{:S(2)}) async-start(), calls=%async_computation.6 | async-start | bytes 1081344 | tf_op jit(solution)/shard_map/all_gather | solution.py:127
  72.4 10.8 %collective-permute-start.2 = (f32[16,16,256]{2,1,0:T(8,128)S(1)}, f32[16,16,256]{2,1,0:T(8,128)S(1)}, u32[]{:S(2)}, u32[]{:S(2)}) collective-permute-start(f32[16,16,256]{2,1,0:T(8,128)S(1)} %all_to_all.30), channel_id=1, source_target_pairs={{0,16},{16,0},{32,48},{48,32},{64,80},{80,64},{96,112},{112,96},{1... | collective-permute-start | bytes 786440 | tf_op jit(solution)/shard_map/ppermute | solution.py:30
  117.2 5.2 %copy-start.3 = (f32[256,256]{1,0:T(8,128)S(1)}, f32[256,256]{1,0:T(8,128)}, u32[]{:S(2)}) copy-start(f32[256,256]{1,0:T(8,128)} %get-tuple-element.7) | copy-start | bytes 786436
  121.0 1.9 copy-start.1
  122.9 3.8 %copy-start = (f32[512,256]{1,0:T(8,128)S(1)}, f32[512,256]{1,0:T(8,128)}, u32[]{:S(2)}) copy-start(f32[512,256]{1,0:T(8,128)} %param.2) | copy-start | bytes 1572868
  148.1 4.1 %collective-permute-start.5 = (f32[16,256]{1,0:T(8,128)S(1)}, f32[16,256]{1,0:T(8,128)S(1)}, u32[]{:S(2)}, u32[]{:S(2)}) collective-permute-start(f32[16,256]{1,0:T(8,128)S(1)} %slice.47), channel_id=1, source_target_pairs={{0,16},{16,0},{32,48},{48,32},{64,80},{80,64},{96,112},{112,96},{1... | collective-permute-start | bytes 49160 | tf_op jit(solution)/shard_map/ppermute | solution.py:30
  152.9 21.9 %all-to-all-start.4 = ((f32[16,16,256]{2,1,0:T(8,128)}), f32[16,16,256]{2,1,0:T(8,128)S(1)}, u32[]{:S(2)}, u32[]{:S(2)}) async-start(f32[16,16,256]{2,1,0:T(8,128)} %broadcast_in_dim.23), calls=%async_computation.4 | async-start | bytes 524288 | tf_op jit(solution)/shard_map/all_to_all | solution.py:42
  175.8 14.2 %all-to-all-start.5 = ((f32[16,48,256]{2,1,0:T(8,128)}), f32[16,48,256]{2,1,0:T(8,128)S(1)}, u32[]{:S(2)}, u32[]{:S(2)}) async-start(f32[16,48,256]{2,1,0:T(8,128)} %broadcast_in_dim.44), calls=%async_computation.5 | async-start | bytes 1572864 | tf_op jit(solution)/shard_map/all_to_all | solution.py:42
  179.4 27.8 %copy-start.4 = (f32[256,256]{1,0:T(8,128)S(1)}, f32[256,256]{1,0:T(8,128)}, u32[]{:S(2)}) copy-start(f32[256,256]{1,0:T(8,128)} %get-tuple-element.9) | copy-start | bytes 786436
  179.4 0.8 collective-permute-start.3
  190.8 37.1 %all-to-all-start.3 = ((f32[16,32,256]{2,1,0:T(8,128)}), f32[16,32,256]{2,1,0:T(8,128)S(1)}, u32[]{:S(2)}, u32[]{:S(2)}) async-start(f32[16,32,256]{2,1,0:T(8,128)} %broadcast_in_dim.22), calls=%async_computation.3 | async-start | bytes 1048576 | tf_op jit(solution)/shard_map/all_to_all | solution.py:42
  227.9 11.5 %collective-permute-start.4 = (f32[512,256]{1,0:T(8,128)S(1)}, f32[512,256]{1,0:T(8,128)S(1)}, u32[]{:S(2)}, u32[]{:S(2)}) collective-permute-start(f32[512,256]{1,0:T(8,128)S(1)} %bitcast.42), channel_id=1, source_target_pairs={{0,16},{16,0},{32,48},{48,32},{64,80},{80,64},{96,112},{112,96},{1... | collective-permute-start | bytes 1572872 | tf_op jit(solution)/shard_map/ppermute | solution.py:30
  240.4 1.9 copy-start.2
Sparse Core Ops, SparseCore 0:
  48.8 72.1 all-gather.2

commit v3 on v2

--- a/solution.py
+++ b/solution.py
@@ -36,15 +36,15 @@
     return jnp.where(first, value, other), jnp.where(first, other, value)
 
 
-def spread(value, axis, groups=None):
-    count = lax.axis_size(axis) if groups is None else len(groups[0])
-    copies = jnp.broadcast_to(value[None], (count, *value.shape))
-    return lax.all_to_all(copies, axis, 0, 0, axis_index_groups=groups)
+def spread(value, axis):
+    copies = jnp.broadcast_to(value[None], (lax.axis_size(axis), *value.shape))
+    return lax.all_to_all(copies, axis, 0, 0)
 
 
-def spread_chips(value):
+def gather_chips(value):
     chips = lax.axis_size("row") // 2
-    return spread(value, "row", [[2 * z + k for z in range(chips)] for k in range(2)])
+    groups = [[2 * z + k for z in range(chips)] for k in range(2)]
+    return lax.all_gather(value, "row", axis=0, tiled=False, axis_index_groups=groups)
 
 
 def turn(piece):
@@ -102,7 +102,7 @@
 
 def body(panel, trailing):
     row_count, width = panel.shape
-    rows, cols = lax.axis_size("row"), lax.axis_size("col")
+    cols = lax.axis_size("col")
     row_index = lax.axis_index("row")
     col_index = lax.axis_index("col")
     core = row_index % 2
@@ -122,19 +122,17 @@
     )
     gram_half = cut(gram_here, mine, half_rows) + received[:half_rows]
     top_half = jnp.where(core == 0, cut(panel, mine, half_rows), received[half_rows:])
-    halves = jnp.concatenate([gram_half, top_half], axis=0)
-    halves, turned = lax.optimization_barrier((halves, turned))
-    gathered = lax.all_gather(turned, "row", axis=0, tiled=False)
-    stacked = spread_chips(halves)
-    halves = jnp.concatenate([jnp.sum(stacked[:, :half_rows], axis=0), stacked[0, half_rows:]], axis=0)
+    stacked = gather_chips(jnp.concatenate([turned, gram_half, top_half], axis=0))
+    panel_cols = stacked[:, :piece_rows].reshape(row_count, width)
+    panel_cols = jnp.concatenate(both_cores(panel_cols), axis=0)
+    gram_half = jnp.sum(stacked[:, piece_rows : piece_rows + half_rows], axis=0)
+    halves = jnp.concatenate([gram_half, stacked[0, piece_rows + half_rows :]], axis=0)
     pair = jnp.stack(both_cores(spread(halves, "col")), axis=1)
     gram = pair[:, :, :half_rows].reshape(width, width)
     top_panel = pair[:, :, half_rows:].reshape(width, width)
     upper, middle = factor(gram, top_panel)
     band_block = -upper
 
-    panel_cols = gathered.reshape(rows // 2, 2, piece_rows, width).transpose(1, 0, 2, 3)
-    panel_cols = panel_cols.reshape(rows * piece_rows, width)
     top_add = jnp.pad(upper, ((0, row_count - width), (0, 0)))
     vectors = panel + jnp.where(row_index == 0, top_add, 0.0)
     top_add = jnp.pad(upper, ((0, panel_cols.shape[0] - width), (0, 0)))
@@ -149,12 +147,14 @@
     image_piece = summed[:piece_rows]
     inner_part = summed[piece_rows:]
     image_turned = turn(image_piece)
-    inner_part = jnp.sum(spread_chips(inner_part + swapped(inner_part)), axis=0)
+    inner_part = inner_part + swapped(inner_part)
+    stacked = gather_chips(jnp.concatenate([image_turned, inner_part], axis=0))
+    image_cols = stacked[:, :piece_rows].reshape(row_count, width)
+    image_cols = jnp.concatenate(both_cores(image_cols), axis=0)
+    inner_part = jnp.sum(stacked[:, piece_rows:], axis=0)
     shared = spread(jnp.concatenate([image_piece, inner_part], axis=0), "col")
     image = shared[:, :piece_rows].reshape(row_count, width)
     inner = shared[:, piece_rows:].reshape(width, width)
-    image_cols = spread_chips(image_turned).reshape(row_count, width)
-    image_cols = jnp.concatenate(both_cores(image_cols), axis=0)
 
     half = 0.5 * product_tn(middle, product(inner, middle))
     correction = product(image, middle) - product(vectors, half)

time: 254 us -> 225 us (0.89)
  blocking collectives: 33.9 us -> 111 us
  waiting for transfers between devices: 61.3 us -> 11.2 us
  starting transfers between devices: 84.2 us -> 41.5 us
  between operations: 14.4 us -> 1.03 us
  local copies, waits for them, and re-layouts: 6.83 us -> 3.67 us
    all_gather x0 -> x2, blocking collectives: none -> 79.4 us  [gather_chips(): lax.all_gather(value, 'row', axis=0, tiled=False, axis_index_groups=groups)]
    all_to_all x4 -> x1, starting transfers between devices: 51.1 us -> 4.26 us  [spread(): return lax.all_to_all(copies, axis, 0, 0)]
    all_to_all x4 -> x1, waiting for transfers between devices: 54.9 us -> 11.1 us  [spread(): return lax.all_to_all(copies, axis, 0, 0)]
    ppermute x4 -> x5, starting transfers between devices: 31.6 us -> 35.9 us  [swapped(): lax.ppermute(value, 'row', [(i, i ^ 1) for i in range(lax.axis_size('row'...]
    all_to_all x1, blocking collectives: 20.3 us -> 16.3 us  [body(): summed = jnp.sum(lax.all_to_all(sent, 'col', 0, 0), axis=0)]
    all_gather x1 -> x0, waiting for transfers between devices: 3.75 us -> none  [body(): gathered = lax.all_gather(turned, 'row', axis=0, tiled=False)]
  transfers between devices with their start and end apart: 11 -> 8, of which waited for: 7 -> 2; matrix products, arithmetic and copies ran while one was open for 2% -> 3% of each run, Pallas kernels for 13% -> 15%
where the time goes in v3:
time: 225 us; the launch traced here: 224 us
  blocking collectives  111 us (49%)
  starting transfers between devices  41.5 us (18%)
  Pallas kernels  33.2 us (15%)
  matrix products  17.9 us (8%)
  waiting for transfers between devices  11.2 us (5%)
  other arithmetic  4.64 us (2%)
  local copies, waits for them, and re-layouts  3.67 us (2%)
    all_gather x2, blocking collectives, gather_chips(): lax.all_gather(value, 'row', axis=0, tiled=False, axis_index_groups=groups)  79.4 us
    ppermute x5, starting transfers between devices, swapped(): lax.ppermute(value, 'row', [(i, i ^ 1) for i in range(lax.axis_size('row'...  35.9 us
    pallas_call x1, Pallas kernels, factor(): pl.pallas_call(functools.partial(factor_kernel, block=block), out_shape=(...  33.2 us
    all_to_all x1, blocking collectives, body(): summed = jnp.sum(lax.all_to_all(sent, 'col', 0, 0), axis=0)  16.3 us
    all_to_all x1, blocking collectives, spread(): return lax.all_to_all(copies, axis, 0, 0)  15 us
    all_to_all x1, waiting for transfers between devices, spread(): return lax.all_to_all(copies, axis, 0, 0)  11.1 us
    dot_general x6, matrix products, product(): jnp.dot(left, right, precision=highest, preferred_element_type=jnp.float32)  8.7 us
    dot_general x2, matrix products, product_nt(): lax.dot_general(left, right, (((1,), (1,)), ((), ())), precision=highest,...  5.33 us
  transfers between devices with their start and end apart: 8, of which 2 were waited for; matrix products, arithmetic and copies ran while one was open for 3% of the time, Pallas kernels for 15%

profile of v3, /device:TPU:1, one launch (start us, length us, event | category | flops | bytes accessed | tf_op | source)
XLA Modules:
  0.0 223.9 jit_solution(10817646158069327991)
XLA Ops:
  0.7 2.3 %fusion.18 = f32[256,256]{1,0:T(8,128)S(1)} fusion(f32[512,256]{1,0:T(8,128)} %param.2), kind=kOutput, calls=%fused_computation.48 | convolution fusion | flops 402653184 | bytes 786432 | tf_op jit(solution)/shard_map/dot_general | solution.py:24
  3.0 0.7 constant_dynamic-slice_fusion
  3.7 8.8 %collective-permute-start.1 = (f32[16,256]{1,0:T(8,128)S(1)}, f32[16,256]{1,0:T(8,128)S(1)}, u32[]{:S(2)}, u32[]{:S(2)}) collective-permute-start(f32[16,256]{1,0:T(8,128)S(1)} %pad_maximum_fusion.5), channel_id=1, source_target_pairs={{0,16},{16,0},{32,48},{48,32},{64,80},{80,64},{96,112},{112,96},{1... | collective-permute-start | bytes 49160 | tf_op jit(solution)/shard_map/ppermute | solution.py:30
  12.5 0.8 constant_dynamic-slice_fusion.2
  13.2 0.7 collective-permute-start
  13.9 0.0 collective-permute-done.1
  13.9 0.7 slice_add_fusion
  14.6 0.0 collective-permute-done
  14.6 40.1 %all-gather = f32[768,256]{1,0:T(8,128)S(1)} all-gather(f32[48,256]{1,0:T(8,128)S(1)} %pad_maximum_fusion.2), channel_id=2, replica_groups={{0,32,64,96,128,160,192,224,256,288,320,352,384,416,448,480},{16,48,80,..., dimensions={0}, use_global_device_ids=true | all-gather | bytes 835584 | tf_op jit(solution)/shard_map/all_gather | solution.py:47
  54.8 15.0 %all_to_all.15 = f32[16,16,256]{2,1,0:T(8,128)S(1)} all-to-all(f32[16,16,256]{2,1,0:T(8,128)S(1)} %broadcast_in_dim.20), channel_id=1, replica_groups=mesh['row'=32,'col'=16] {'col'}, dimensions={0} | all-to-all | bytes 524288 | tf_op jit(solution)/shard_map/all_to_all | solution.py:41
  69.8 12.0 %collective-permute-start.2 = (f32[16,16,256]{2,1,0:T(8,128)S(1)}, f32[16,16,256]{2,1,0:T(8,128)S(1)}, u32[]{:S(2)}, u32[]{:S(2)}) collective-permute-start(f32[16,16,256]{2,1,0:T(8,128)S(1)} %all_to_all.15), channel_id=1, source_target_pairs={{0,16},{16,0},{32,48},{48,32},{64,80},{80,64},{96,112},{112,96},{1... | collective-permute-start | bytes 786440 | tf_op jit(solution)/shard_map/ppermute | solution.py:30
  81.8 1.9 collective-permute-start.3
  83.8 0.0 collective-permute-done.2
  83.8 0.8 pad_maximum_fusion.1
  84.7 33.2 %shard_map.41 = (f32[256,256]{1,0:T(8,128)}, f32[256,256]{1,0:T(8,128)}) custom-call(f32[256,256]{1,0:T(8,128)} %bitcast.50, f32[256,256]{1,0:T(8,128)} %bitcast.49), custom_call_target="tpu_custom_call" | custom-call | tf_op jit(solution)/shard_map/pallas_call | solution.py:99
  117.8 0.0 copy-start.1
  117.8 0.0 collective-permute-done.3
  117.8 0.1 broadcast_select_fusion.3
  117.9 0.9 copy-done.1
  118.8 0.0 copy-start
  118.8 5.2 %fusion.7 = f32[256,512]{1,0:T(8,128)S(1)} fusion(f32[512,1024]{1,0:T(8,128)} %param.3, f32[512,256]{1,0:T(8,128)S(1)} %get-tuple-element.9, f32[512,256]{1,0:T(8,128)S(1)} %get-tuple-element.8, f32[256,256]{1,0:T(8,128)S(1)} %copy-done.1, pred[]{:T(512)S(6)} %eq.19), kind=kOutput, calls=%fused_computation.28 | convolution fusion | flops 1611399168 | bytes 3932161 | tf_op jit(solution)/shard_map/dot_general | solution.py:14
  124.0 0.2 copy.7
  124.2 0.0 copy-done
  124.2 1.0 fusion.5
  125.2 0.1 pad_maximum_fusion
  125.3 16.3 %all_to_all.16 = f32[16,48,256]{2,1,0:T(8,128)S(1)} all-to-all(f32[16,48,256]{2,1,0:T(8,128)S(1)} %pad_maximum_fusion), channel_id=1, replica_groups=mesh['row'=32,'col'=16] {'col'}, dimensions={0} | all-to-all | bytes 1572864 | tf_op jit(solution)/shard_map/all_to_all | solution.py:146
  141.6 0.1 reduce_sum.28
  141.6 3.5 %collective-permute-start.5 = (f32[16,256]{1,0:T(8,128)S(1)}, f32[16,256]{1,0:T(8,128)S(1)}, u32[]{:S(2)}, u32[]{:S(2)}) collective-permute-start(f32[16,256]{1,0:T(8,128)S(1)} %slice.60), channel_id=1, source_target_pairs={{0,16},{16,0},{32,48},{48,32},{64,80},{80,64},{96,112},{112,96},{1... | collective-permute-start | bytes 49160 | tf_op jit(solution)/shard_map/ppermute | solution.py:30
  145.2 0.7 collective-permute-start.4
  145.9 0.1 collective-permute-done.5
  146.0 0.0 collective-permute-done.4
  146.0 39.3 %all-gather.1 = f32[768,256]{1,0:T(8,128)S(1)} all-gather(f32[48,256]{1,0:T(8,128)S(1)} %pad_maximum_fusion.3), channel_id=3, replica_groups={{0,32,64,96,128,160,192,224,256,288,320,352,384,416,448,480},{16,48,80,..., dimensions={0}, use_global_device_ids=true | all-gather | bytes 835584 | tf_op jit(solution)/shard_map/all_gather | solution.py:47
  185.4 9.8 %collective-permute-start.6 = (f32[512,256]{1,0:T(8,128)S(1)}, f32[512,256]{1,0:T(8,128)}, u32[]{:S(2)}, u32[]{:S(2)}) collective-permute-start(f32[512,256]{1,0:T(8,128)S(1)} %bitcast.45), channel_id=1, source_target_pairs={{0,16},{16,0},{32,48},{48,32},{64,80},{80,64},{96,112},{112,96},{1... | collective-permute-start | bytes 1572872 | tf_op jit(solution)/shard_map/ppermute | solution.py:30
  195.2 1.0 broadcast_in_dim.23
  196.1 4.3 %all-to-all-start.2 = ((f32[16,48,256]{2,1,0:T(8,128)}), f32[16,48,256]{2,1,0:T(8,128)S(1)}, u32[]{:S(2)}, u32[]{:S(2)}) async-start(f32[16,48,256]{2,1,0:T(8,128)} %broadcast_in_dim.23), calls=%async_computation.2 | async-start | bytes 1572864 | tf_op jit(solution)/shard_map/all_to_all | solution.py:41
  200.4 0.0 copy-start.3
  200.4 0.7 neg.3
  201.1 0.0 collective-permute-done.6
  201.1 2.1 broadcast_select_fusion.1
  203.2 11.1 %all-to-all-done.2 = f32[16,48,256]{2,1,0:T(8,128)S(1)} async-done(((f32[16,48,256]{2,1,0:T(8,128)}), f32[16,48,256]{2,1,0:T(8,128)S(1)}, u32[]{:S(2)}, u32[]{:S(2)}) %all-to-all-start.2) | async-done | bytes 786464 | tf_op jit(solution)/shard_map/all_to_all | solution.py:41
  214.3 0.0 copy-done.3
  214.3 0.6 fusion.20
  214.9 0.4 fusion.19
  215.3 0.6 convolution_multiply_fusion
  215.9 0.0 copy-start.4
  215.9 0.0 copy-start.5
  215.9 1.0 fusion.6
  216.9 0.6 convolution_subtract_fusion.1
  217.5 0.0 copy-done.4
  217.5 0.0 copy-done.5
  217.6 1.0 convolution_subtract_fusion
  218.6 0.0 copy-start.2
  218.6 1.9 fusion.4
  220.4 0.0 copy-done.2
  220.5 3.5 %subtract_subtract_fusion = f32[512,1024]{1,0:T(8,128)} fusion(f32[512,1024]{1,0:T(8,128)S(1)} %copy-done.2, f32[512,1024]{1,0:T(8,128)S(1)} %fusion.4, f32[512,256]{1,0:T(8,128)S(1)} %convolution_subtract_fusion.1, f32[512,256]{1,0:T(8,128)S(1)} %get-tuple-element.9, f32[512,256]{1,0:T(8,128)S(1)} %get-tuple-element.8, f32[256,256]{1,0:T(8,128)S(1)} %copy-done.1, ...), kind=kOutput, calls=%fused_computation | convolution fusion | flops 1612447744 | bytes 8126465 | tf_op jit(solution)/shard_map/dot_general | solution.py:18
  (17 shorter events, 0.3 us)
Async XLA Ops:
  3.7 10.2 %collective-permute-start.1 = (f32[16,256]{1,0:T(8,128)S(1)}, f32[16,256]{1,0:T(8,128)S(1)}, u32[]{:S(2)}, u32[]{:S(2)}) collective-permute-start(f32[16,256]{1,0:T(8,128)S(1)} %pad_maximum_fusion.5), channel_id=1, source_target_pairs={{0,16},{16,0},{32,48},{48,32},{64,80},{80,64},{96,112},{112,96},{1... | collective-permute-start | bytes 49160 | tf_op jit(solution)/shard_map/ppermute | solution.py:30
  13.2 1.4 collective-permute-start
  69.8 13.9 %collective-permute-start.2 = (f32[16,16,256]{2,1,0:T(8,128)S(1)}, f32[16,16,256]{2,1,0:T(8,128)S(1)}, u32[]{:S(2)}, u32[]{:S(2)}) collective-permute-start(f32[16,16,256]{2,1,0:T(8,128)S(1)} %all_to_all.15), channel_id=1, source_target_pairs={{0,16},{16,0},{32,48},{48,32},{64,80},{80,64},{96,112},{112,96},{1... | collective-permute-start | bytes 786440 | tf_op jit(solution)/shard_map/ppermute | solution.py:30
  81.8 36.0 %collective-permute-start.3 = (f32[512,256]{1,0:T(8,128)S(1)}, f32[512,256]{1,0:T(8,128)S(1)}, u32[]{:S(2)}, u32[]{:S(2)}) collective-permute-start(f32[512,256]{1,0:T(8,128)S(1)} %bitcast.44), channel_id=1, source_target_pairs={{0,16},{16,0},{32,48},{48,32},{64,80},{80,64},{96,112},{112,96},{1... | collective-permute-start | bytes 1572872 | tf_op jit(solution)/shard_map/ppermute | solution.py:30
  117.8 0.9 copy-start.1
  118.8 5.4 %copy-start = (f32[512,256]{1,0:T(8,128)S(1)}, f32[512,256]{1,0:T(8,128)}, u32[]{:S(2)}) copy-start(f32[512,256]{1,0:T(8,128)} %param.2) | copy-start | bytes 1572868
  141.6 4.4 %collective-permute-start.5 = (f32[16,256]{1,0:T(8,128)S(1)}, f32[16,256]{1,0:T(8,128)S(1)}, u32[]{:S(2)}, u32[]{:S(2)}) collective-permute-start(f32[16,256]{1,0:T(8,128)S(1)} %slice.60), channel_id=1, source_target_pairs={{0,16},{16,0},{32,48},{48,32},{64,80},{80,64},{96,112},{112,96},{1... | collective-permute-start | bytes 49160 | tf_op jit(solution)/shard_map/ppermute | solution.py:30
  145.2 0.8 collective-permute-start.4
  185.4 15.7 %collective-permute-start.6 = (f32[512,256]{1,0:T(8,128)S(1)}, f32[512,256]{1,0:T(8,128)}, u32[]{:S(2)}, u32[]{:S(2)}) collective-permute-start(f32[512,256]{1,0:T(8,128)S(1)} %bitcast.45), channel_id=1, source_target_pairs={{0,16},{16,0},{32,48},{48,32},{64,80},{80,64},{96,112},{112,96},{1... | collective-permute-start | bytes 1572872 | tf_op jit(solution)/shard_map/ppermute | solution.py:30
  196.1 18.1 %all-to-all-start.2 = ((f32[16,48,256]{2,1,0:T(8,128)}), f32[16,48,256]{2,1,0:T(8,128)S(1)}, u32[]{:S(2)}, u32[]{:S(2)}) async-start(f32[16,48,256]{2,1,0:T(8,128)} %broadcast_in_dim.23), calls=%async_computation.2 | async-start | bytes 1572864 | tf_op jit(solution)/shard_map/all_to_all | solution.py:41
  200.4 13.9 %copy-start.3 = (f32[256,256]{1,0:T(8,128)S(1)}, f32[256,256]{1,0:T(8,128)}, u32[]{:S(2)}) copy-start(f32[256,256]{1,0:T(8,128)} %get-tuple-element.5) | copy-start | bytes 786436
  215.9 1.6 copy-start.4
  215.9 1.6 copy-start.5
  218.6 1.9 copy-start.2

commit v4 on v3

v4 whole, which is shorter than its diff:
```python
import functools

import jax
import jax.numpy as jnp
from jax import lax
from jax.experimental import pallas as pl
from jax.experimental.pallas import tpu as pltpu
from jax.sharding import PartitionSpec as P

highest = lax.Precision.HIGHEST
high = lax.Precision.HIGH


def product(left, right, precision=highest):
    return jnp.dot(left, right, precision=precision, preferred_element_type=jnp.float32)


def product_nt(left, right, precision=highest):
    return lax.dot_general(
        left,
        right,
        (((1,), (1,)), ((), ())),
        precision=precision,
        preferred_element_type=jnp.float32,
    )


def product_tn(left, right):
    return lax.dot_general(
        left, right, (((0,), (0,)), ((), ())), precision=highest, preferred_element_type=jnp.float32
    )


def swapped(value):
    return lax.ppermute(value, "row", [(i, i ^ 1) for i in range(lax.axis_size("row"))])


def both_cores(value):
    other = swapped(value)
    first = lax.axis_index("row") % 2 == 0
    return jnp.where(first, value, other), jnp.where(first, other, value)


def spread(value, own):
    copies = jnp.broadcast_to(value[None], (own.shape[0], *value.shape))
    return lax.all_to_all(jnp.concatenate([own, copies], axis=1), "col", 0, 0)


def gather_chips(value):
    chips = lax.axis_size("row") // 2
    groups = [[2 * z + k for z in range(chips)] for k in range(2)]
    return lax.all_gather(value, "row", axis=0, tiled=False, axis_index_groups=groups)


lanes = 128


def tiled(value, width):
    return jnp.concatenate([value] * (width // lanes), axis=1)


class Sweep:
    def __init__(self, panel, start, below, sub):
        self.panel, self.start, self.below, self.sub = panel, start, below, sub
        self.rows = panel.shape[0]
        self.place = lax.broadcasted_iota(jnp.int32, (self.rows, lanes), 0)
        self.pivots = jnp.zeros((self.rows, lanes), jnp.float32)

    def step(self, j):
        k = j % self.sub
        if k == 0:
            self.columns = [
                jnp.broadcast_to(self.panel[:, self.start + j + i : self.start + j + i + 1], (self.rows, lanes))
                for i in range(self.sub)
            ]
        column = self.columns[k]
        pivot = column[j : j + 1]
        keep = self.place > j if self.below else self.place != j
        ratio = jnp.where(keep, column * (1.0 / pivot), 0.0)
        for i in range(k + 1, self.sub):
            self.columns[i] = self.columns[i] - ratio * self.columns[i][j : j + 1]
        self.panel = self.panel - tiled(ratio, self.panel.shape[1]) * self.panel[j : j + 1]
        self.pivots = jnp.where(self.place == j, pivot, self.pivots)


def factor_kernel(gram_ref, top_ref, upper_ref, middle_ref, left, right, *, block, sub):
    width = gram_ref.shape[0]
    rows = lax.broadcasted_iota(jnp.int32, (width, width), 0)
    cols = lax.broadcasted_iota(jnp.int32, (width, width), 1)
    left[:, :width] = gram_ref[...]
    left[:, width:] = jnp.where(rows == cols, 1.0, 0.0)
    right[:, :width] = top_ref[...]
    right[:, width:] = jnp.zeros((width, width), jnp.float32)
    wide_row = lax.broadcasted_iota(jnp.int32, (block, 2 * width), 0)
    wide_col = lax.broadcasted_iota(jnp.int32, (block, 2 * width), 1)
    all_rows = lax.broadcasted_iota(jnp.int32, (width, block), 0)
    side = None
    for start in range(0, width + block, block):
        stop = start + block
        sweeps = []
        if start < width:
            sweeps.append(Sweep(left[start:stop, :], start, True, sub))
        if start:
            sweeps.append(Sweep(side, start - block, False, sub))
        for j in range(block):
            for sweep in sweeps:
                sweep.step(j)
        if start:
            old = start - block
            side = sweeps[-1].panel * tiled(1.0 / sweeps[-1].pivots, 2 * width)
            others = jnp.where((all_rows < old) | (all_rows >= start), right[:, old:start], 0.0)
            right[...] = right[...] - product(others, side)
            right[old:start, :] = side
        if start < width:
            pivots = sweeps[0].pivots
            scale = lax.rsqrt(pivots)
            scale = scale * (1.5 - 0.5 * pivots * scale * scale)
            part = jnp.where(wide_col >= wide_row + start, sweeps[0].panel * tiled(scale, 2 * width), 0.0)
            upper_ref[start:stop, :] = part[:, :width]
            if stop < width:
                left[stop:, :] = left[stop:, :] - product_tn(part[:, stop:width], part)
            side = right[start:stop, :] + part
    middle_ref[...] = right[:, width:]


def factor(gram, top):
    width = gram.shape[0]
    square = jax.ShapeDtypeStruct((width, width), jnp.float32)
    return pl.pallas_call(
        functools.partial(factor_kernel, block=64, sub=8),
        out_shape=(square, square),
        scratch_shapes=[pltpu.VMEM((width, 2 * width), jnp.float32)] * 2,
    )(gram, top)


def body(panel, trailing):
    row_count, width = panel.shape
    cols = lax.axis_size("col")
    row_index = lax.axis_index("row")
    col_index = lax.axis_index("col")
    core = row_index % 2
    piece_rows = row_count // cols
    part_rows = width // cols
    half_rows = part_rows // 2

    def cut(value, start, size):
        return lax.dynamic_slice_in_dim(value, start, size, 0)

    panel_piece = cut(panel, col_index * piece_rows, piece_rows)
    gram_here = product_tn(panel, panel)
    mine = col_index * part_rows + core * half_rows
    theirs = col_index * part_rows + (1 - core) * half_rows
    received = swapped(
        jnp.concatenate([cut(gram_here, theirs, half_rows), cut(panel, theirs, half_rows)], axis=0)
    )
    gram_half = cut(gram_here, mine, half_rows) + received[:half_rows]
    top_half = jnp.where(core == 0, cut(panel, mine, half_rows), received[half_rows:])
    stacked = gather_chips(jnp.concatenate([panel_piece, gram_half, top_half], axis=0))
    gram_half = jnp.sum(stacked[:, piece_rows : piece_rows + half_rows], axis=0)
    halves = jnp.concatenate([gram_half, stacked[0, piece_rows + half_rows :]], axis=0)
    received = spread(halves, stacked[:, :piece_rows])
    pair = jnp.stack(both_cores(received[:, piece_rows:]), axis=1)
    gram = pair[:, :, :half_rows].reshape(width, width)
    top_panel = pair[:, :, half_rows:].reshape(width, width)
    panel_cols = received[:, :piece_rows].reshape(row_count, width)
    panel_cols = jnp.concatenate(both_cores(panel_cols), axis=0)
    upper, middle = factor(gram, top_panel)
    band_block = -upper

    top_add = jnp.pad(upper, ((0, row_count - width), (0, 0)))
    vectors = panel + jnp.where(row_index == 0, top_add, 0.0)
    top_add = jnp.pad(upper, ((0, panel_cols.shape[0] - width), (0, 0)))
    vector_cols = panel_cols + jnp.where(col_index == 0, top_add, 0.0)

    partial = product(trailing, vector_cols, high)
    inner = product_tn(vectors, partial)
    sent = jnp.concatenate(
        [partial.reshape(cols, piece_rows, width), inner.reshape(cols, part_rows, width)], axis=1
    )
    summed = jnp.sum(lax.all_to_all(sent, "col", 0, 0), axis=0)
    image_piece = summed[:piece_rows]
    inner_part = summed[piece_rows:]
    inner_part = inner_part + swapped(inner_part)
    stacked = gather_chips(jnp.concatenate([image_piece, inner_part], axis=0))
    inner_part = jnp.sum(stacked[:, piece_rows:], axis=0)
    received = spread(
        jnp.concatenate([image_piece, inner_part], axis=0), stacked[:, :piece_rows]
    )
    image_cols = received[:, :piece_rows].reshape(row_count, width)
    image_cols = jnp.concatenate(both_cores(image_cols), axis=0)
    image = received[:, piece_rows : 2 * piece_rows].reshape(row_count, width)
    inner = received[:, 2 * piece_rows :].reshape(width, width)

    half = 0.5 * product_tn(middle, product(inner, middle))
    correction = product(image, middle) - product(vectors, half)
    correction_cols = product(image_cols, middle) - product(vector_cols, half)
    updated = (
        trailing
        - product_nt(vectors, correction_cols, high)
        - product_nt(correction, vector_cols, high)
    )
    return (band_block, updated)


def solution(mesh):
    in_specs = (P("row", None), P("row", "col"))
    out_specs = (P(), P("row", "col"))
    return jax.shard_map(body, mesh=mesh, in_specs=in_specs, out_specs=out_specs, check_vma=False)
```

time: 225 us -> 177 us (0.79)
  blocking collectives: 111 us -> 84.8 us
  Pallas kernels: 33.2 us -> 15.9 us
  matrix products: 17.9 us -> 14.5 us
  waiting for transfers between devices: 11.2 us -> 14.5 us
  starting transfers between devices: 41.5 us -> 38.6 us
    all_gather x2, blocking collectives: 79.4 us -> 51.6 us  [gather_chips(): lax.all_gather(value, 'row', axis=0, tiled=False, axis_index_groups=groups)]
    pallas_call x1, Pallas kernels: 33.2 us -> 15.9 us  [factor(): pl.pallas_call(functools.partial(factor_kernel, block=64, sub=8), out_sha...]
    dot_general x8, matrix products: 14 us -> 10.7 us  [the longest x6 7.02 us: product(): jnp.dot(left, right, precision=precision, preferred_element_type=jnp.floa...]
    all_to_all x1, waiting for transfers between devices: 11.1 us -> 13.6 us  [spread(): return lax.all_to_all(jnp.concatenate([own, copies], axis=1), 'col', 0, 0)]
  transfers between devices with their start and end apart: 8 -> 6, of which waited for: 2 -> 2; matrix products, arithmetic and copies ran while one was open for 3% -> 2% of each run, Pallas kernels for 15% -> 9%
where the time goes in v4:
time: 177 us
  blocking collectives  84.8 us (48%)
  starting transfers between devices  38.6 us (22%)
  Pallas kernels  15.9 us (9%)
  matrix products  14.5 us (8%)
  waiting for transfers between devices  14.5 us (8%)
  other arithmetic  3.86 us (2%)
  local copies, waits for them, and re-layouts  3.42 us (2%)
    all_gather x2, blocking collectives, gather_chips(): lax.all_gather(value, 'row', axis=0, tiled=False, axis_index_groups=groups)  51.6 us
    ppermute x5, starting transfers between devices, swapped(): lax.ppermute(value, 'row', [(i, i ^ 1) for i in range(lax.axis_size('row'...  34.8 us
    all_to_all x1, blocking collectives, spread(): return lax.all_to_all(jnp.concatenate([own, copies], axis=1), 'col', 0, 0)  16.9 us
    all_to_all x1, blocking collectives, body(): summed = jnp.sum(lax.all_to_all(sent, 'col', 0, 0), axis=0)  16.3 us
    pallas_call x1, Pallas kernels, factor(): pl.pallas_call(functools.partial(factor_kernel, block=64, sub=8), out_sha...  15.9 us
    all_to_all x1, waiting for transfers between devices, spread(): return lax.all_to_all(jnp.concatenate([own, copies], axis=1), 'col', 0, 0)  13.6 us
    dot_general x6, matrix products, product(): jnp.dot(left, right, precision=precision, preferred_element_type=jnp.floa...  7.02 us
    all_to_all x1, starting transfers between devices, spread(): return lax.all_to_all(jnp.concatenate([own, copies], axis=1), 'col', 0, 0)  3.83 us
  transfers between devices with their start and end apart: 6, of which 2 were waited for; matrix products, arithmetic and copies ran while one was open for 2% of the time, Pallas kernels for 9%

profile of v4, /device:TPU:1, one launch (start us, length us, event | category | flops | bytes accessed | tf_op | source)
XLA Modules:
  0.0 176.6 jit_solution(10100385140206387264)
XLA Ops:
  0.7 2.2 %fusion.19 = f32[256,256]{1,0:T(8,128)S(1)} fusion(f32[512,256]{1,0:T(8,128)} %param.2), kind=kOutput, calls=%fused_computation.51 | convolution fusion | flops 402653184 | bytes 786432 | tf_op jit(solution)/shard_map/dot_general | solution.py:29
  2.9 0.7 constant_dynamic-slice_fusion
  3.6 8.8 %collective-permute-start = (f32[16,256]{1,0:T(8,128)S(1)}, f32[16,256]{1,0:T(8,128)S(1)}, u32[]{:S(2)}, u32[]{:S(2)}) collective-permute-start(f32[16,256]{1,0:T(8,128)S(1)} %pad_maximum_fusion.7), channel_id=1, source_target_pairs={{0,16},{16,0},{32,48},{48,32},{64,80},{80,64},{96,112},{112,96},{1... | collective-permute-start | bytes 49160 | tf_op jit(solution)/shard_map/ppermute | solution.py:35
  12.4 0.8 constant_dynamic-slice_fusion.2
  13.1 0.0 collective-permute-done
  13.2 0.7 slice_add_fusion
  13.9 27.8 %all-gather = f32[768,256]{1,0:T(8,128)S(1)} all-gather(f32[48,256]{1,0:T(8,128)S(1)} %pad_maximum_fusion.6), channel_id=2, replica_groups={{0,32,64,96,128,160,192,224,256,288,320,352,384,416,448,480},{16,48,80,..., dimensions={0}, use_global_device_ids=true | all-gather | bytes 835584 | tf_op jit(solution)/shard_map/all_gather | solution.py:52
  41.8 0.1 pad_maximum_fusion.1
  41.9 16.9 %all_to_all.15 = f32[16,48,256]{2,1,0:T(8,128)S(1)} all-to-all(f32[16,48,256]{2,1,0:T(8,128)S(1)} %pad_maximum_fusion.1), channel_id=1, replica_groups=mesh['row'=32,'col'=16] {'col'}, dimensions={0} | all-to-all | bytes 1572864 | tf_op jit(solution)/shard_map/all_to_all | solution.py:46
  58.8 10.3 %collective-permute-start.1 = (f32[16,16,256]{2,1,0:T(8,128)S(1)}, f32[16,16,256]{2,1,0:T(8,128)S(1)}, u32[]{:S(2)}, u32[]{:S(2)}) collective-permute-start(f32[16,16,256]{2,1,0:T(8,128)S(1)} %slice.69), channel_id=1, source_target_pairs={{0,16},{16,0},{32,48},{48,32},{64,80},{80,64},{96,112},{112,96},{1... | collective-permute-start | bytes 786440 | tf_op jit(solution)/shard_map/ppermute | solution.py:35
  69.2 1.9 %collective-permute-start.2 = (f32[512,256]{1,0:T(8,128)S(1)}, f32[512,256]{1,0:T(8,128)S(1)}, u32[]{:S(2)}, u32[]{:S(2)}) collective-permute-start(f32[512,256]{1,0:T(8,128)S(1)} %bitcast.44), channel_id=1, source_target_pairs={{0,16},{16,0},{32,48},{48,32},{64,80},{80,64},{96,112},{112,96},{1... | collective-permute-start | bytes 1572872 | tf_op jit(solution)/shard_map/ppermute | solution.py:35
  71.1 0.0 collective-permute-done.1
  71.2 0.8 pad_maximum_fusion.3
  72.0 15.9 %shard_map.41 = (f32[256,256]{1,0:T(8,128)}, f32[256,256]{1,0:T(8,128)}) custom-call(f32[256,256]{1,0:T(8,128)} %bitcast.50, f32[256,256]{1,0:T(8,128)} %bitcast.49), custom_call_target="tpu_custom_call" | custom-call | tf_op jit(solution)/shard_map/pallas_call | solution.py:129
  87.9 0.0 copy-start.1
  87.9 0.0 collective-permute-done.2
  87.9 0.1 broadcast_select_fusion.3
  88.0 0.9 copy-done.1
  88.9 0.0 copy-start
  88.9 3.5 %fusion.7 = f32[256,512]{1,0:T(8,128)S(1)} fusion(f32[512,1024]{1,0:T(8,128)} %param.3, f32[512,256]{1,0:T(8,128)S(1)} %get-tuple-element.11, f32[512,256]{1,0:T(8,128)S(1)} %get-tuple-element.10, f32[256,256]{1,0:T(8,128)S(1)} %copy-done.1, pred[]{:T(512)S(6)} %eq.19), kind=kOutput, calls=%fused_computation.30 | convolution fusion | flops 806092800 | bytes 3932161 | tf_op jit(solution)/shard_map/dot_general | solution.py:15
  92.4 0.2 copy.7
  92.6 0.0 copy-done
  92.6 1.0 fusion.5
  93.6 0.1 pad_maximum_fusion.2
  93.7 16.3 %all_to_all.16 = f32[16,48,256]{2,1,0:T(8,128)S(1)} all-to-all(f32[16,48,256]{2,1,0:T(8,128)S(1)} %pad_maximum_fusion.2), channel_id=1, replica_groups=mesh['row'=32,'col'=16] {'col'}, dimensions={0} | all-to-all | bytes 1572864 | tf_op jit(solution)/shard_map/all_to_all | solution.py:180
  110.0 0.1 reduce_sum.28
  110.0 3.5 %collective-permute-start.3 = (f32[16,256]{1,0:T(8,128)S(1)}, f32[16,256]{1,0:T(8,128)S(1)}, u32[]{:S(2)}, u32[]{:S(2)}) collective-permute-start(f32[16,256]{1,0:T(8,128)S(1)} %slice.74), channel_id=1, source_target_pairs={{0,16},{16,0},{32,48},{48,32},{64,80},{80,64},{96,112},{112,96},{1... | collective-permute-start | bytes 49160 | tf_op jit(solution)/shard_map/ppermute | solution.py:35
  113.6 0.8 collective-permute-done.3
  114.4 23.8 %all-gather.1 = f32[768,256]{1,0:T(8,128)S(1)} all-gather(f32[48,256]{1,0:T(8,128)S(1)} %pad_maximum_fusion.5), channel_id=3, replica_groups={{0,32,64,96,128,160,192,224,256,288,320,352,384,416,448,480},{16,48,80,..., dimensions={0}, use_global_device_ids=true | all-gather | bytes 835584 | tf_op jit(solution)/shard_map/all_gather | solution.py:52
  138.3 0.1 broadcast_in_dim.23
  138.4 1.2 pad_maximum_fusion
  139.5 0.0 copy-start.3
  139.5 3.8 %all-to-all-start.2 = ((f32[16,80,256]{2,1,0:T(8,128)}), f32[16,80,256]{2,1,0:T(8,128)S(1)}, u32[]{:S(2)}, u32[]{:S(2)}) async-start(f32[16,80,256]{2,1,0:T(8,128)} %pad_maximum_fusion), calls=%async_computation.2 | async-start | bytes 2621440 | tf_op jit(solution)/shard_map/all_to_all | solution.py:46
  143.4 0.7 neg.3
  144.1 13.6 %all-to-all-done.2 = f32[16,80,256]{2,1,0:T(8,128)S(1)} async-done(((f32[16,80,256]{2,1,0:T(8,128)}), f32[16,80,256]{2,1,0:T(8,128)S(1)}, u32[]{:S(2)}, u32[]{:S(2)}) %all-to-all-start.2) | async-done | bytes 1310752 | tf_op jit(solution)/shard_map/all_to_all | solution.py:46
  157.7 0.1 fusion.18
  157.8 0.0 copy-done.3
  157.8 0.6 fusion.21
  158.4 0.4 fusion.20
  158.8 0.6 convolution_multiply_fusion
  159.4 10.2 %collective-permute-start.4 = (f32[512,256]{1,0:T(8,128)S(1)}, f32[512,256]{1,0:T(8,128)S(1)}, u32[]{:S(2)}, u32[]{:S(2)}) collective-permute-start(f32[512,256]{1,0:T(8,128)S(1)} %bitcast.46), channel_id=1, source_target_pairs={{0,16},{16,0},{32,48},{48,32},{64,80},{80,64},{96,112},{112,96},{1... | collective-permute-start | bytes 1572872 | tf_op jit(solution)/shard_map/ppermute | solution.py:35
  169.7 1.0 fusion.6
  170.7 0.6 convolution_subtract_fusion.1
  171.3 0.0 collective-permute-done.4
  171.3 0.1 broadcast_select_fusion.1
  171.4 1.0 convolution_subtract_fusion
  172.4 0.0 copy-start.2
  172.4 1.0 fusion.4
  173.4 0.5 copy-done.2
  174.0 2.6 %subtract_subtract_fusion = f32[512,1024]{1,0:T(8,128)} fusion(f32[512,1024]{1,0:T(8,128)S(1)} %copy-done.2, f32[512,1024]{1,0:T(8,128)S(1)} %fusion.4, f32[512,256]{1,0:T(8,128)S(1)} %convolution_subtract_fusion.1, f32[512,256]{1,0:T(8,128)S(1)} %get-tuple-element.11, f32[512,256]{1,0:T(8,128)S(1)} %get-tuple-element.10, f32[256,256]{1,0:T(8,128)S(1)} %copy-done.1, ...), kind=kOutput, calls=%fused_computation | convolution fusion | flops 807141376 | bytes 8126465 | tf_op jit(solution)/shard_map/dot_general | solution.py:19
  (18 shorter events, 0.3 us)
Async XLA Ops:
  3.6 9.6 %collective-permute-start = (f32[16,256]{1,0:T(8,128)S(1)}, f32[16,256]{1,0:T(8,128)S(1)}, u32[]{:S(2)}, u32[]{:S(2)}) collective-permute-start(f32[16,256]{1,0:T(8,128)S(1)} %pad_maximum_fusion.7), channel_id=1, source_target_pairs={{0,16},{16,0},{32,48},{48,32},{64,80},{80,64},{96,112},{112,96},{1... | collective-permute-start | bytes 49160 | tf_op jit(solution)/shard_map/ppermute | solution.py:35
  58.8 12.3 %collective-permute-start.1 = (f32[16,16,256]{2,1,0:T(8,128)S(1)}, f32[16,16,256]{2,1,0:T(8,128)S(1)}, u32[]{:S(2)}, u32[]{:S(2)}) collective-permute-start(f32[16,16,256]{2,1,0:T(8,128)S(1)} %slice.69), channel_id=1, source_target_pairs={{0,16},{16,0},{32,48},{48,32},{64,80},{80,64},{96,112},{112,96},{1... | collective-permute-start | bytes 786440 | tf_op jit(solution)/shard_map/ppermute | solution.py:35
  69.2 18.7 %collective-permute-start.2 = (f32[512,256]{1,0:T(8,128)S(1)}, f32[512,256]{1,0:T(8,128)S(1)}, u32[]{:S(2)}, u32[]{:S(2)}) collective-permute-start(f32[512,256]{1,0:T(8,128)S(1)} %bitcast.44), channel_id=1, source_target_pairs={{0,16},{16,0},{32,48},{48,32},{64,80},{80,64},{96,112},{112,96},{1... | collective-permute-start | bytes 1572872 | tf_op jit(solution)/shard_map/ppermute | solution.py:35
  87.9 0.9 copy-start.1
  88.9 3.7 %copy-start = (f32[512,256]{1,0:T(8,128)S(1)}, f32[512,256]{1,0:T(8,128)}, u32[]{:S(2)}) copy-start(f32[512,256]{1,0:T(8,128)} %param.2) | copy-start | bytes 1572868
  110.0 4.4 %collective-permute-start.3 = (f32[16,256]{1,0:T(8,128)S(1)}, f32[16,256]{1,0:T(8,128)S(1)}, u32[]{:S(2)}, u32[]{:S(2)}) collective-permute-start(f32[16,256]{1,0:T(8,128)S(1)} %slice.74), channel_id=1, source_target_pairs={{0,16},{16,0},{32,48},{48,32},{64,80},{80,64},{96,112},{112,96},{1... | collective-permute-start | bytes 49160 | tf_op jit(solution)/shard_map/ppermute | solution.py:35
  139.5 18.3 %copy-start.3 = (f32[256,256]{1,0:T(8,128)S(1)}, f32[256,256]{1,0:T(8,128)}, u32[]{:S(2)}) copy-start(f32[256,256]{1,0:T(8,128)} %get-tuple-element.5) | copy-start | bytes 786436
  139.5 18.2 %all-to-all-start.2 = ((f32[16,80,256]{2,1,0:T(8,128)}), f32[16,80,256]{2,1,0:T(8,128)S(1)}, u32[]{:S(2)}, u32[]{:S(2)}) async-start(f32[16,80,256]{2,1,0:T(8,128)} %pad_maximum_fusion), calls=%async_computation.2 | async-start | bytes 2621440 | tf_op jit(solution)/shard_map/all_to_all | solution.py:46
  159.4 11.8 %collective-permute-start.4 = (f32[512,256]{1,0:T(8,128)S(1)}, f32[512,256]{1,0:T(8,128)S(1)}, u32[]{:S(2)}, u32[]{:S(2)}) collective-permute-start(f32[512,256]{1,0:T(8,128)S(1)} %bitcast.46), channel_id=1, source_target_pairs={{0,16},{16,0},{32,48},{48,32},{64,80},{80,64},{96,112},{112,96},{1... | collective-permute-start | bytes 1572872 | tf_op jit(solution)/shard_map/ppermute | solution.py:35
  172.4 1.6 copy-start.2

commit v5 on v4

--- a/solution.py
+++ b/solution.py
@@ -91,35 +91,47 @@
     left[:, width:] = jnp.where(rows == cols, 1.0, 0.0)
     right[:, :width] = top_ref[...]
     right[:, width:] = jnp.zeros((width, width), jnp.float32)
-    wide_row = lax.broadcasted_iota(jnp.int32, (block, 2 * width), 0)
-    wide_col = lax.broadcasted_iota(jnp.int32, (block, 2 * width), 1)
+    span = width + width // 2
+    wide_row = lax.broadcasted_iota(jnp.int32, (block, span), 0)
+    wide_col = lax.broadcasted_iota(jnp.int32, (block, span), 1)
     all_rows = lax.broadcasted_iota(jnp.int32, (width, block), 0)
+
+    def window(start):
+        return 0 if start < width // 2 else width // 2
+
     side = None
     for start in range(0, width + block, block):
         stop = start + block
+        low = window(start)
+        high_end = low + span
+        old = start - block
         sweeps = []
         if start < width:
-            sweeps.append(Sweep(left[start:stop, :], start, True, sub))
+            sweeps.append(Sweep(left[start:stop, low:high_end], start - low, True, sub))
         if start:
-            sweeps.append(Sweep(side, start - block, False, sub))
+            sweeps.append(Sweep(side, old - window(old), False, sub))
         for j in range(block):
             for sweep in sweeps:
                 sweep.step(j)
         if start:
-            old = start - block
-            side = sweeps[-1].panel * tiled(1.0 / sweeps[-1].pivots, 2 * width)
+            side = sweeps[-1].panel * tiled(1.0 / sweeps[-1].pivots, span)
             others = jnp.where((all_rows < old) | (all_rows >= start), right[:, old:start], 0.0)
-            right[...] = right[...] - product(others, side)
-            right[old:start, :] = side
+            place = slice(window(old), window(old) + span)
+            right[:, place] = right[:, place] - product(others, side)
+            right[old:start, place] = side
         if start < width:
             pivots = sweeps[0].pivots
             scale = lax.rsqrt(pivots)
             scale = scale * (1.5 - 0.5 * pivots * scale * scale)
-            part = jnp.where(wide_col >= wide_row + start, sweeps[0].panel * tiled(scale, 2 * width), 0.0)
-            upper_ref[start:stop, :] = part[:, :width]
+            part = sweeps[0].panel * tiled(scale, span)
+            part = jnp.where(wide_col + low >= wide_row + start, part, 0.0)
+            if low:
+                upper_ref[start:stop, :low] = jnp.zeros((block, low), jnp.float32)
+            upper_ref[start:stop, low:] = part[:, : width - low]
             if stop < width:
-                left[stop:, :] = left[stop:, :] - product_tn(part[:, stop:width], part)
-            side = right[start:stop, :] + part
+                trail = product_tn(part[:, stop - low : width - low], part)
+                left[stop:, low:high_end] = left[stop:, low:high_end] - trail
+            side = right[start:stop, low:high_end] + part
     middle_ref[...] = right[:, width:]
 
 
@@ -180,25 +192,23 @@
     summed = jnp.sum(lax.all_to_all(sent, "col", 0, 0), axis=0)
     image_piece = summed[:piece_rows]
     inner_part = summed[piece_rows:]
-    inner_part = inner_part + swapped(inner_part)
     stacked = gather_chips(jnp.concatenate([image_piece, inner_part], axis=0))
     inner_part = jnp.sum(stacked[:, piece_rows:], axis=0)
     received = spread(
-        jnp.concatenate([image_piece, inner_part], axis=0), stacked[:, :piece_rows]
-    )
-    image_cols = received[:, :piece_rows].reshape(row_count, width)
-    image_cols = jnp.concatenate(both_cores(image_cols), axis=0)
-    image = received[:, piece_rows : 2 * piece_rows].reshape(row_count, width)
-    inner = received[:, 2 * piece_rows :].reshape(width, width)
+        jnp.concatenate([inner_part, image_piece], axis=0), stacked[:, :piece_rows]
+    )
+    split = piece_rows + part_rows
+    image = received[:, split:].reshape(row_count, width)
+    first, second = both_cores(received[:, :split])
+    inner = (first[:, piece_rows:] + second[:, piece_rows:]).reshape(width, width)
+    image_cols = jnp.stack([first[:, :piece_rows], second[:, :piece_rows]])
+    image_cols = image_cols.reshape(2 * row_count, width)
 
     half = 0.5 * product_tn(middle, product(inner, middle))
     correction = product(image, middle) - product(vectors, half)
+    updated = trailing - product_nt(correction, vector_cols, high)
     correction_cols = product(image_cols, middle) - product(vector_cols, half)
-    updated = (
-        trailing
-        - product_nt(vectors, correction_cols, high)
-        - product_nt(correction, vector_cols, high)
-    )
+    updated = updated - product_nt(vectors, correction_cols, high)
     return (band_block, updated)
 
 

time: 177 us -> 173 us (0.977)
  blocking collectives: 84.8 us -> 102 us
  waiting for transfers between devices: 14.5 us -> 0.58 us
  starting transfers between devices: 38.6 us -> 32.2 us
    all_to_all x1 -> x2, blocking collectives: 16.9 us -> 34.1 us  [spread(): return lax.all_to_all(jnp.concatenate([own, copies], axis=1), 'col', 0, 0)]
    all_to_all x1 -> x0, waiting for transfers between devices: 13.6 us -> none  [spread(): return lax.all_to_all(jnp.concatenate([own, copies], axis=1), 'col', 0, 0)]
    all_to_all x1 -> x0, starting transfers between devices: 3.83 us -> none  [spread(): return lax.all_to_all(jnp.concatenate([own, copies], axis=1), 'col', 0, 0)]
    ppermute x5 -> x4, starting transfers between devices: 34.8 us -> 32.2 us  [swapped(): lax.ppermute(value, 'row', [(i, i ^ 1) for i in range(lax.axis_size('row'...]
  transfers between devices with their start and end apart: 6 -> 4, of which waited for: 2 -> 1; matrix products, arithmetic and copies ran while one was open for 2% -> 2% of each run, Pallas kernels for 9% -> 9%
where the time goes in v5:
time: 173 us; the launch traced here: 172 us
  blocking collectives  102 us (59%)
  starting transfers between devices  32.2 us (19%)
  Pallas kernels  15.5 us (9%)
  matrix products  14.4 us (8%)
  local copies, waits for them, and re-layouts  3.47 us (2%)
  other arithmetic  2.97 us (2%)
    all_gather x2, blocking collectives, gather_chips(): lax.all_gather(value, 'row', axis=0, tiled=False, axis_index_groups=groups)  51.7 us
    all_to_all x2, blocking collectives, spread(): return lax.all_to_all(jnp.concatenate([own, copies], axis=1), 'col', 0, 0)  34.1 us
    ppermute x4, starting transfers between devices, swapped(): lax.ppermute(value, 'row', [(i, i ^ 1) for i in range(lax.axis_size('row'...  32.2 us
    all_to_all x1, blocking collectives, body(): summed = jnp.sum(lax.all_to_all(sent, 'col', 0, 0), axis=0)  16.3 us
    pallas_call x1, Pallas kernels, factor(): pl.pallas_call(functools.partial(factor_kernel, block=64, sub=8), out_sha...  15.5 us
    dot_general x6, matrix products, product(): jnp.dot(left, right, precision=precision, preferred_element_type=jnp.floa...  7.03 us
    dot_general x3, matrix products, product_tn(): lax.dot_general(left, right, (((0,), (0,)), ((), ())), precision=highest,...  3.81 us
    dot_general x2, matrix products, product_nt(): lax.dot_general(left, right, (((1,), (1,)), ((), ())), precision=precisio...  3.6 us
  transfers between devices with their start and end apart: 4, of which 1 were waited for; matrix products, arithmetic and copies ran while one was open for 2% of the time, Pallas kernels for 9%

profile of v5, /device:TPU:1, one launch (start us, length us, event | category | flops | bytes accessed | tf_op | source)
XLA Modules:
  0.0 172.1 jit_solution(8349553069678129840)
XLA Ops:
  0.7 2.2 %fusion.13 = f32[256,256]{1,0:T(8,128)S(1)} fusion(f32[512,256]{1,0:T(8,128)} %param.2), kind=kOutput, calls=%fused_computation.47 | convolution fusion | flops 402653184 | bytes 786432 | tf_op jit(solution)/shard_map/dot_general | solution.py:29
  2.9 0.7 constant_dynamic-slice_fusion
  3.6 8.8 %collective-permute-start = (f32[16,256]{1,0:T(8,128)S(1)}, f32[16,256]{1,0:T(8,128)S(1)}, u32[]{:S(2)}, u32[]{:S(2)}) collective-permute-start(f32[16,256]{1,0:T(8,128)S(1)} %pad_maximum_fusion.7), channel_id=1, source_target_pairs={{0,16},{16,0},{32,48},{48,32},{64,80},{80,64},{96,112},{112,96},{1... | collective-permute-start | bytes 49160 | tf_op jit(solution)/shard_map/ppermute | solution.py:35
  12.4 0.8 constant_dynamic-slice_fusion.2
  13.1 0.0 collective-permute-done
  13.2 0.7 slice_add_fusion.1
  13.9 27.8 %all-gather = f32[768,256]{1,0:T(8,128)S(1)} all-gather(f32[48,256]{1,0:T(8,128)S(1)} %pad_maximum_fusion.5), channel_id=2, replica_groups={{0,32,64,96,128,160,192,224,256,288,320,352,384,416,448,480},{16,48,80,..., dimensions={0}, use_global_device_ids=true | all-gather | bytes 835584 | tf_op jit(solution)/shard_map/all_gather | solution.py:52
  41.8 0.1 pad_maximum_fusion.2
  41.9 16.9 %all_to_all.15 = f32[16,48,256]{2,1,0:T(8,128)S(1)} all-to-all(f32[16,48,256]{2,1,0:T(8,128)S(1)} %pad_maximum_fusion.2), channel_id=1, replica_groups=mesh['row'=32,'col'=16] {'col'}, dimensions={0} | all-to-all | bytes 1572864 | tf_op jit(solution)/shard_map/all_to_all | solution.py:46
  58.8 10.3 %collective-permute-start.1 = (f32[16,16,256]{2,1,0:T(8,128)S(1)}, f32[16,16,256]{2,1,0:T(8,128)S(1)}, u32[]{:S(2)}, u32[]{:S(2)}) collective-permute-start(f32[16,16,256]{2,1,0:T(8,128)S(1)} %slice.79), channel_id=1, source_target_pairs={{0,16},{16,0},{32,48},{48,32},{64,80},{80,64},{96,112},{112,96},{1... | collective-permute-start | bytes 786440 | tf_op jit(solution)/shard_map/ppermute | solution.py:35
  69.2 1.9 %collective-permute-start.2 = (f32[512,256]{1,0:T(8,128)S(1)}, f32[512,256]{1,0:T(8,128)S(1)}, u32[]{:S(2)}, u32[]{:S(2)}) collective-permute-start(f32[512,256]{1,0:T(8,128)S(1)} %bitcast.48), channel_id=1, source_target_pairs={{0,16},{16,0},{32,48},{48,32},{64,80},{80,64},{96,112},{112,96},{1... | collective-permute-start | bytes 1572872 | tf_op jit(solution)/shard_map/ppermute | solution.py:35
  71.1 0.0 collective-permute-done.1
  71.2 0.8 pad_maximum_fusion.4
  72.0 15.5 %shard_map.41 = (f32[256,256]{1,0:T(8,128)}, f32[256,256]{1,0:T(8,128)}) custom-call(f32[256,256]{1,0:T(8,128)} %bitcast.53, f32[256,256]{1,0:T(8,128)} %bitcast.52), custom_call_target="tpu_custom_call" | custom-call | tf_op jit(solution)/shard_map/pallas_call | solution.py:141
  87.5 0.0 copy-start.1
  87.5 0.0 collective-permute-done.2
  87.5 0.1 broadcast_select_fusion.3
  87.6 0.9 copy-done.1
  88.4 0.0 copy-start
  88.4 3.5 %fusion.3 = f32[256,512]{1,0:T(8,128)S(1)} fusion(f32[512,1024]{1,0:T(8,128)} %param.3, f32[512,256]{1,0:T(8,128)S(1)} %get-tuple-element.9, f32[512,256]{1,0:T(8,128)S(1)} %get-tuple-element.8, f32[256,256]{1,0:T(8,128)S(1)} %copy-done.1, pred[]{:T(512)S(6)} %eq.18), kind=kOutput, calls=%fused_computation.29 | convolution fusion | flops 806092800 | bytes 3932161 | tf_op jit(solution)/shard_map/dot_general | solution.py:15
  92.0 0.2 copy.9
  92.2 0.0 copy-done
  92.2 1.0 fusion.2
  93.2 0.1 pad_maximum_fusion.3
  93.2 16.3 %all_to_all.16 = f32[16,48,256]{2,1,0:T(8,128)S(1)} all-to-all(f32[16,48,256]{2,1,0:T(8,128)S(1)} %pad_maximum_fusion.3), channel_id=1, replica_groups=mesh['row'=32,'col'=16] {'col'}, dimensions={0} | all-to-all | bytes 1572864 | tf_op jit(solution)/shard_map/all_to_all | solution.py:192
  109.6 0.1 reduce_sum.28
  109.6 23.9 %all-gather.1 = f32[768,256]{1,0:T(8,128)S(1)} all-gather(f32[48,256]{1,0:T(8,128)S(1)} %reduce_sum.28), channel_id=3, replica_groups={{0,32,64,96,128,160,192,224,256,288,320,352,384,416,448,480},{16,48,80,..., dimensions={0}, use_global_device_ids=true | all-gather | bytes 835584 | tf_op jit(solution)/shard_map/all_gather | solution.py:52
  133.6 0.1 broadcast_in_dim.23
  133.7 0.1 pad_maximum_fusion
  133.8 17.1 %all_to_all.17 = f32[16,80,256]{2,1,0:T(8,128)S(1)} all-to-all(f32[16,80,256]{2,1,0:T(8,128)S(1)} %pad_maximum_fusion), channel_id=1, replica_groups=mesh['row'=32,'col'=16] {'col'}, dimensions={0} | all-to-all | bytes 2621440 | tf_op jit(solution)/shard_map/all_to_all | solution.py:46
  150.9 0.0 copy-start.3
  150.9 0.1 slice.87
  151.0 11.2 %collective-permute-start.3 = (f32[16,48,256]{2,1,0:T(8,128)S(1)}, f32[16,48,256]{2,1,0:T(8,128)S(1)}, u32[]{:S(2)}, u32[]{:S(2)}) collective-permute-start(f32[16,48,256]{2,1,0:T(8,128)S(1)} %slice.87), channel_id=1, source_target_pairs={{0,16},{16,0},{32,48},{48,32},{64,80},{80,64},{96,112},{112,96},{1... | collective-permute-start | bytes 2359304 | tf_op jit(solution)/shard_map/ppermute | solution.py:35
  162.1 0.7 neg.3
  162.9 0.0 copy-done.3
  162.9 0.6 fusion.14
  163.5 0.5 collective-permute-done.3
  164.0 0.1 broadcast_select_fusion.1
  164.3 0.4 fusion.15
  164.7 0.6 convolution_multiply_fusion
  165.3 0.1 pad_maximum_fusion.1
  165.4 1.0 fusion.16
  166.4 0.6 convolution_subtract_fusion.1
  167.0 1.0 convolution_subtract_fusion
  168.0 0.0 copy-start.2
  168.0 1.0 fusion.1
  169.0 0.5 copy-done.2
  169.6 2.6 %subtract_subtract_fusion = f32[512,1024]{1,0:T(8,128)} fusion(f32[512,1024]{1,0:T(8,128)S(1)} %fusion.1, f32[512,1024]{1,0:T(8,128)S(1)} %copy-done.2, f32[512,256]{1,0:T(8,128)S(1)} %convolution_subtract_fusion.1, f32[512,256]{1,0:T(8,128)S(1)} %get-tuple-element.9, f32[512,256]{1,0:T(8,128)S(1)} %get-tuple-element.8, f32[256,256]{1,0:T(8,128)S(1)} %copy-done.1, ...), kind=kOutput, calls=%fused_computation | convolution fusion | flops 807141376 | bytes 8126465 | tf_op jit(solution)/shard_map/dot_general | solution.py:19
  (18 shorter events, 0.4 us)
Async XLA Ops:
  3.6 9.6 %collective-permute-start = (f32[16,256]{1,0:T(8,128)S(1)}, f32[16,256]{1,0:T(8,128)S(1)}, u32[]{:S(2)}, u32[]{:S(2)}) collective-permute-start(f32[16,256]{1,0:T(8,128)S(1)} %pad_maximum_fusion.7), channel_id=1, source_target_pairs={{0,16},{16,0},{32,48},{48,32},{64,80},{80,64},{96,112},{112,96},{1... | collective-permute-start | bytes 49160 | tf_op jit(solution)/shard_map/ppermute | solution.py:35
  58.8 12.3 %collective-permute-start.1 = (f32[16,16,256]{2,1,0:T(8,128)S(1)}, f32[16,16,256]{2,1,0:T(8,128)S(1)}, u32[]{:S(2)}, u32[]{:S(2)}) collective-permute-start(f32[16,16,256]{2,1,0:T(8,128)S(1)} %slice.79), channel_id=1, source_target_pairs={{0,16},{16,0},{32,48},{48,32},{64,80},{80,64},{96,112},{112,96},{1... | collective-permute-start | bytes 786440 | tf_op jit(solution)/shard_map/ppermute | solution.py:35
  69.2 18.3 %collective-permute-start.2 = (f32[512,256]{1,0:T(8,128)S(1)}, f32[512,256]{1,0:T(8,128)S(1)}, u32[]{:S(2)}, u32[]{:S(2)}) collective-permute-start(f32[512,256]{1,0:T(8,128)S(1)} %bitcast.48), channel_id=1, source_target_pairs={{0,16},{16,0},{32,48},{48,32},{64,80},{80,64},{96,112},{112,96},{1... | collective-permute-start | bytes 1572872 | tf_op jit(solution)/shard_map/ppermute | solution.py:35
  87.5 0.9 copy-start.1
  88.4 3.7 %copy-start = (f32[512,256]{1,0:T(8,128)S(1)}, f32[512,256]{1,0:T(8,128)}, u32[]{:S(2)}) copy-start(f32[512,256]{1,0:T(8,128)} %param.2) | copy-start | bytes 1572868
  150.9 12.0 %copy-start.3 = (f32[256,256]{1,0:T(8,128)S(1)}, f32[256,256]{1,0:T(8,128)}, u32[]{:S(2)}) copy-start(f32[256,256]{1,0:T(8,128)} %get-tuple-element.5) | copy-start | bytes 786436
  151.0 13.0 %collective-permute-start.3 = (f32[16,48,256]{2,1,0:T(8,128)S(1)}, f32[16,48,256]{2,1,0:T(8,128)S(1)}, u32[]{:S(2)}, u32[]{:S(2)}) collective-permute-start(f32[16,48,256]{2,1,0:T(8,128)S(1)} %slice.87), channel_id=1, source_target_pairs={{0,16},{16,0},{32,48},{48,32},{64,80},{80,64},{96,112},{112,96},{1... | collective-permute-start | bytes 2359304 | tf_op jit(solution)/shard_map/ppermute | solution.py:35
  168.0 1.6 copy-start.2

commit v6 on v5

--- a/solution.py
+++ b/solution.py
@@ -171,11 +171,12 @@
     gram_half = jnp.sum(stacked[:, piece_rows : piece_rows + half_rows], axis=0)
     halves = jnp.concatenate([gram_half, stacked[0, piece_rows + half_rows :]], axis=0)
     received = spread(halves, stacked[:, :piece_rows])
-    pair = jnp.stack(both_cores(received[:, piece_rows:]), axis=1)
-    gram = pair[:, :, :half_rows].reshape(width, width)
-    top_panel = pair[:, :, half_rows:].reshape(width, width)
-    panel_cols = received[:, :piece_rows].reshape(row_count, width)
-    panel_cols = jnp.concatenate(both_cores(panel_cols), axis=0)
+    first, second = both_cores(received)
+    pair = jnp.stack([first, second], axis=1)
+    gram = pair[:, :, piece_rows : piece_rows + half_rows].reshape(width, width)
+    top_panel = pair[:, :, piece_rows + half_rows :].reshape(width, width)
+    panel_cols = jnp.stack([first[:, :piece_rows], second[:, :piece_rows]])
+    panel_cols = panel_cols.reshape(2 * row_count, width)
     upper, middle = factor(gram, top_panel)
     band_block = -upper
 
@@ -204,10 +205,9 @@
     image_cols = jnp.stack([first[:, :piece_rows], second[:, :piece_rows]])
     image_cols = image_cols.reshape(2 * row_count, width)
 
-    half = 0.5 * product_tn(middle, product(inner, middle))
-    correction = product(image, middle) - product(vectors, half)
-    updated = trailing - product_nt(correction, vector_cols, high)
-    correction_cols = product(image_cols, middle) - product(vector_cols, half)
+    updated = trailing - product_nt(product(image, middle), vector_cols, high)
+    core_square = product_tn(middle, product(inner, middle))
+    correction_cols = product(image_cols, middle) - product(vector_cols, core_square)
     updated = updated - product_nt(vectors, correction_cols, high)
     return (band_block, updated)
 

time: 173 us -> 172 us (level)
  starting transfers between devices: 32.2 us -> 30.1 us
    ppermute x4 -> x3, starting transfers between devices: 32.2 us -> 30.1 us  [swapped(): lax.ppermute(value, 'row', [(i, i ^ 1) for i in range(lax.axis_size('row'...]
    dot_general x6 -> x5, matrix products: 7.03 us -> 6.48 us  [product(): jnp.dot(left, right, precision=precision, preferred_element_type=jnp.floa...]
  transfers between devices with their start and end apart: 4 -> 3, of which waited for: 1 -> 1; matrix products, arithmetic and copies ran while one was open for 2% -> 2% of each run, Pallas kernels for 9% -> 0%
where the time goes in v6:
time: 172 us; the launch traced here: 171 us
  blocking collectives  102 us (59%)
  starting transfers between devices  30.1 us (18%)
  Pallas kernels  15.5 us (9%)
  matrix products  14 us (8%)
  other arithmetic  4.17 us (2%)
  local copies, waits for them, and re-layouts  2.64 us (2%)
  waiting for transfers between devices  1.93 us (1%)
    all_gather x2, blocking collectives, gather_chips(): lax.all_gather(value, 'row', axis=0, tiled=False, axis_index_groups=groups)  51.9 us
    all_to_all x2, blocking collectives, spread(): return lax.all_to_all(jnp.concatenate([own, copies], axis=1), 'col', 0, 0)  33.8 us
    ppermute x3, starting transfers between devices, swapped(): lax.ppermute(value, 'row', [(i, i ^ 1) for i in range(lax.axis_size('row'...  30.1 us
    all_to_all x1, blocking collectives, body(): summed = jnp.sum(lax.all_to_all(sent, 'col', 0, 0), axis=0)  16.4 us
    pallas_call x1, Pallas kernels, factor(): pl.pallas_call(functools.partial(factor_kernel, block=64, sub=8), out_sha...  15.5 us
    dot_general x5, matrix products, product(): jnp.dot(left, right, precision=precision, preferred_element_type=jnp.floa...  6.48 us
    dot_general x3, matrix products, product_tn(): lax.dot_general(left, right, (((0,), (0,)), ((), ())), precision=highest,...  3.81 us
    dot_general x2, matrix products, product_nt(): lax.dot_general(left, right, (((1,), (1,)), ((), ())), precision=precisio...  3.67 us
  transfers between devices with their start and end apart: 3, of which 1 were waited for; matrix products, arithmetic and copies ran while one was open for 2% of the time, Pallas kernels for 0%

profile of v6, /device:TPU:1, one launch (start us, length us, event | category | flops | bytes accessed | tf_op | source)
XLA Modules:
  0.0 171.5 jit_solution(1490896091722765654)
XLA Ops:
  0.7 2.2 %fusion.7 = f32[256,256]{1,0:T(8,128)S(1)} fusion(f32[512,256]{1,0:T(8,128)} %param.2), kind=kOutput, calls=%fused_computation.39 | convolution fusion | flops 402653184 | bytes 786432 | tf_op jit(solution)/shard_map/dot_general | solution.py:29
  2.9 0.7 constant_dynamic-slice_fusion
  3.6 8.8 %collective-permute-start = (f32[16,256]{1,0:T(8,128)S(1)}, f32[16,256]{1,0:T(8,128)S(1)}, u32[]{:S(2)}, u32[]{:S(2)}) collective-permute-start(f32[16,256]{1,0:T(8,128)S(1)} %pad_maximum_fusion.9), channel_id=1, source_target_pairs={{0,16},{16,0},{32,48},{48,32},{64,80},{80,64},{96,112},{112,96},{1... | collective-permute-start | bytes 49160 | tf_op jit(solution)/shard_map/ppermute | solution.py:35
  12.4 0.8 constant_dynamic-slice_fusion.2
  13.1 0.0 collective-permute-done
  13.2 0.7 slice_add_fusion.1
  13.9 27.8 %all-gather = f32[768,256]{1,0:T(8,128)S(1)} all-gather(f32[48,256]{1,0:T(8,128)S(1)} %pad_maximum_fusion.7), channel_id=2, replica_groups={{0,32,64,96,128,160,192,224,256,288,320,352,384,416,448,480},{16,48,80,..., dimensions={0}, use_global_device_ids=true | all-gather | bytes 835584 | tf_op jit(solution)/shard_map/all_gather | solution.py:52
  41.8 0.1 pad_maximum_fusion.3
  41.9 16.9 %all_to_all.15 = f32[16,48,256]{2,1,0:T(8,128)S(1)} all-to-all(f32[16,48,256]{2,1,0:T(8,128)S(1)} %pad_maximum_fusion.3), channel_id=1, replica_groups=mesh['row'=32,'col'=16] {'col'}, dimensions={0} | all-to-all | bytes 1572864 | tf_op jit(solution)/shard_map/all_to_all | solution.py:46
  58.8 10.3 %collective-permute-start.1 = (f32[16,48,256]{2,1,0:T(8,128)S(1)}, f32[16,48,256]{2,1,0:T(8,128)S(1)}, u32[]{:S(2)}, u32[]{:S(2)}) collective-permute-start(f32[16,48,256]{2,1,0:T(8,128)S(1)} %all_to_all.15), channel_id=1, source_target_pairs={{0,16},{16,0},{32,48},{48,32},{64,80},{80,64},{96,112},{112,96},{1... | collective-permute-start | bytes 2359304 | tf_op jit(solution)/shard_map/ppermute | solution.py:35
  69.1 1.9 %collective-permute-done.1 = f32[16,48,256]{2,1,0:T(8,128)S(1)} collective-permute-done((f32[16,48,256]{2,1,0:T(8,128)S(1)}, f32[16,48,256]{2,1,0:T(8,128)S(1)}, u32[]{:S(2)}, u32[]{:S(2)}) %collective-permute-start.1) | collective-permute-done | bytes 786464 | tf_op jit(solution)/shard_map/ppermute | solution.py:35
  71.0 0.1 broadcast_select_fusion.3
  71.2 0.1 pad_maximum_fusion.1
  71.3 0.8 pad_maximum_fusion.5
  72.1 15.5 %shard_map.41 = (f32[256,256]{1,0:T(8,128)}, f32[256,256]{1,0:T(8,128)}) custom-call(f32[256,256]{1,0:T(8,128)} %bitcast.58, f32[256,256]{1,0:T(8,128)} %bitcast.57), custom_call_target="tpu_custom_call" | custom-call | tf_op jit(solution)/shard_map/pallas_call | solution.py:141
  87.6 1.1 bitcast_add_fusion
  88.8 0.0 copy-start
  88.8 0.0 copy-start.3
  88.8 3.5 %fusion.8 = f32[256,512]{1,0:T(8,128)S(1)} fusion(f32[1024,256]{1,0:T(8,128)S(1)} %bitcast_add_fusion, f32[512,1024]{1,0:T(8,128)} %param.3), kind=kOutput, calls=%fused_computation.40 | convolution fusion | flops 805306368 | bytes 3670016 | tf_op jit(solution)/shard_map/dot_general | solution.py:15
  92.3 0.2 copy.7
  92.5 0.0 copy-done
  92.5 0.0 copy-done.3
  92.5 1.0 fusion
  93.5 0.1 pad_maximum_fusion.4
  93.6 16.4 %all_to_all.16 = f32[16,48,256]{2,1,0:T(8,128)S(1)} all-to-all(f32[16,48,256]{2,1,0:T(8,128)S(1)} %pad_maximum_fusion.4), channel_id=1, replica_groups=mesh['row'=32,'col'=16] {'col'}, dimensions={0} | all-to-all | bytes 1572864 | tf_op jit(solution)/shard_map/all_to_all | solution.py:193
  110.0 0.1 reduce_sum.28
  110.1 24.1 %all-gather.1 = f32[768,256]{1,0:T(8,128)S(1)} all-gather(f32[48,256]{1,0:T(8,128)S(1)} %reduce_sum.28), channel_id=3, replica_groups={{0,32,64,96,128,160,192,224,256,288,320,352,384,416,448,480},{16,48,80,..., dimensions={0}, use_global_device_ids=true | all-gather | bytes 835584 | tf_op jit(solution)/shard_map/all_gather | solution.py:52
  134.3 0.1 broadcast_in_dim.23
  134.4 0.1 pad_maximum_fusion
  134.5 16.9 %all_to_all.17 = f32[16,80,256]{2,1,0:T(8,128)S(1)} all-to-all(f32[16,80,256]{2,1,0:T(8,128)S(1)} %pad_maximum_fusion), channel_id=1, replica_groups=mesh['row'=32,'col'=16] {'col'}, dimensions={0} | all-to-all | bytes 2621440 | tf_op jit(solution)/shard_map/all_to_all | solution.py:46
  151.4 0.0 copy-start.2
  151.4 0.1 slice.85
  151.4 11.0 %collective-permute-start.2 = (f32[16,48,256]{2,1,0:T(8,128)S(1)}, f32[16,48,256]{2,1,0:T(8,128)S(1)}, u32[]{:S(2)}, u32[]{:S(2)}) collective-permute-start(f32[16,48,256]{2,1,0:T(8,128)S(1)} %slice.85), channel_id=1, source_target_pairs={{0,16},{16,0},{32,48},{48,32},{64,80},{80,64},{96,112},{112,96},{1... | collective-permute-start | bytes 2359304 | tf_op jit(solution)/shard_map/ppermute | solution.py:35
  162.5 0.7 neg.3
  163.2 0.0 copy-done.2
  163.2 0.6 fusion.9
  163.8 1.0 fusion.10
  164.9 0.0 collective-permute-done.2
  164.9 0.1 broadcast_select_fusion.1
  165.2 0.4 fusion.12
  165.5 0.6 fusion.13
  166.1 0.1 pad_maximum_fusion.2
  166.2 1.0 fusion.11
  167.2 0.0 copy-start.1
  167.3 1.0 convolution_subtract_fusion
  168.3 0.6 copy-done.1
  168.8 2.6 %subtract_subtract_fusion = f32[512,1024]{1,0:T(8,128)} fusion(f32[512,1024]{1,0:T(8,128)S(1)} %copy-done.1, f32[512,1024]{1,0:T(8,128)S(1)} %fusion.10, f32[1024,256]{1,0:T(8,128)S(1)} %convolution_subtract_fusion, f32[512,256]{1,0:T(8,128)S(1)} %copy-done, f32[256,256]{1,0:T(8,128)S(1)} %copy-done.3, pred[]{:T(512)S(6)} %eq.17), kind=kOutput, calls=%fused_computation | convolution fusion | flops 806617088 | bytes 8126465 | tf_op jit(solution)/shard_map/dot_general | solution.py:19
  (17 shorter events, 0.4 us)
Async XLA Ops:
  3.6 9.6 %collective-permute-start = (f32[16,256]{1,0:T(8,128)S(1)}, f32[16,256]{1,0:T(8,128)S(1)}, u32[]{:S(2)}, u32[]{:S(2)}) collective-permute-start(f32[16,256]{1,0:T(8,128)S(1)} %pad_maximum_fusion.9), channel_id=1, source_target_pairs={{0,16},{16,0},{32,48},{48,32},{64,80},{80,64},{96,112},{112,96},{1... | collective-permute-start | bytes 49160 | tf_op jit(solution)/shard_map/ppermute | solution.py:35
  58.8 12.2 %collective-permute-start.1 = (f32[16,48,256]{2,1,0:T(8,128)S(1)}, f32[16,48,256]{2,1,0:T(8,128)S(1)}, u32[]{:S(2)}, u32[]{:S(2)}) collective-permute-start(f32[16,48,256]{2,1,0:T(8,128)S(1)} %all_to_all.15), channel_id=1, source_target_pairs={{0,16},{16,0},{32,48},{48,32},{64,80},{80,64},{96,112},{112,96},{1... | collective-permute-start | bytes 2359304 | tf_op jit(solution)/shard_map/ppermute | solution.py:35
  88.8 3.7 %copy-start = (f32[512,256]{1,0:T(8,128)S(1)}, f32[512,256]{1,0:T(8,128)}, u32[]{:S(2)}) copy-start(f32[512,256]{1,0:T(8,128)} %param.2) | copy-start | bytes 1572868
  88.8 3.7 %copy-start.3 = (f32[256,256]{1,0:T(8,128)S(1)}, f32[256,256]{1,0:T(8,128)}, u32[]{:S(2)}) copy-start(f32[256,256]{1,0:T(8,128)} %get-tuple-element.4) | copy-start | bytes 786436
  151.4 11.9 %copy-start.2 = (f32[256,256]{1,0:T(8,128)S(1)}, f32[256,256]{1,0:T(8,128)}, u32[]{:S(2)}) copy-start(f32[256,256]{1,0:T(8,128)} %get-tuple-element.5) | copy-start | bytes 786436
  151.4 13.5 %collective-permute-start.2 = (f32[16,48,256]{2,1,0:T(8,128)S(1)}, f32[16,48,256]{2,1,0:T(8,128)S(1)}, u32[]{:S(2)}, u32[]{:S(2)}) collective-permute-start(f32[16,48,256]{2,1,0:T(8,128)S(1)} %slice.85), channel_id=1, source_target_pairs={{0,16},{16,0},{32,48},{48,32},{64,80},{80,64},{96,112},{112,96},{1... | collective-permute-start | bytes 2359304 | tf_op jit(solution)/shard_map/ppermute | solution.py:35
  167.2 1.6 copy-start.1

commit v7 on v6

--- a/solution.py
+++ b/solution.py
@@ -205,9 +205,11 @@
     image_cols = jnp.stack([first[:, :piece_rows], second[:, :piece_rows]])
     image_cols = image_cols.reshape(2 * row_count, width)
 
-    updated = trailing - product_nt(product(image, middle), vector_cols, high)
+    updated = trailing - product_nt(product(image, middle, high), vector_cols, high)
     core_square = product_tn(middle, product(inner, middle))
-    correction_cols = product(image_cols, middle) - product(vector_cols, core_square)
+    correction_cols = product(image_cols, middle, high) - product(
+        vector_cols, core_square, high
+    )
     updated = updated - product_nt(vectors, correction_cols, high)
     return (band_block, updated)
 

time: 172 us -> 171 us (level)
  no operation moved by 1% of the time
where the time goes in v7:
time: 171 us
  blocking collectives  102 us (60%)
  starting transfers between devices  30.1 us (18%)
  Pallas kernels  15.5 us (9%)
  matrix products  12.9 us (8%)
  other arithmetic  4.17 us (2%)
  local copies, waits for them, and re-layouts  3.07 us (2%)
  waiting for transfers between devices  1.93 us (1%)
    all_gather x2, blocking collectives, gather_chips(): lax.all_gather(value, 'row', axis=0, tiled=False, axis_index_groups=groups)  51.9 us
    all_to_all x2, blocking collectives, spread(): return lax.all_to_all(jnp.concatenate([own, copies], axis=1), 'col', 0, 0)  33.8 us
    ppermute x3, starting transfers between devices, swapped(): lax.ppermute(value, 'row', [(i, i ^ 1) for i in range(lax.axis_size('row'...  30.1 us
    all_to_all x1, blocking collectives, body(): summed = jnp.sum(lax.all_to_all(sent, 'col', 0, 0), axis=0)  16.4 us
    pallas_call x1, Pallas kernels, factor(): pl.pallas_call(functools.partial(factor_kernel, block=64, sub=8), out_sha...  15.5 us
    dot_general x5, matrix products, product(): jnp.dot(left, right, precision=precision, preferred_element_type=jnp.floa...  5.44 us
    dot_general x3, matrix products, product_tn(): lax.dot_general(left, right, (((0,), (0,)), ((), ())), precision=highest,...  3.81 us
    dot_general x2, matrix products, product_nt(): lax.dot_general(left, right, (((1,), (1,)), ((), ())), precision=precisio...  3.67 us
  transfers between devices with their start and end apart: 3, of which 1 were waited for; matrix products, arithmetic and copies ran while one was open for 2% of the time, Pallas kernels for 0%

profile of v7, /device:TPU:1, one launch (start us, length us, event | category | flops | bytes accessed | tf_op | source)
XLA Modules:
  0.0 170.9 jit_solution(572484406732468670)
XLA Ops:
  0.7 2.2 %fusion.7 = f32[256,256]{1,0:T(8,128)S(1)} fusion(f32[512,256]{1,0:T(8,128)} %param.2), kind=kOutput, calls=%fused_computation.39 | convolution fusion | flops 402653184 | bytes 786432 | tf_op jit(solution)/shard_map/dot_general | solution.py:29
  2.9 0.7 constant_dynamic-slice_fusion
  3.6 8.8 %collective-permute-start = (f32[16,256]{1,0:T(8,128)S(1)}, f32[16,256]{1,0:T(8,128)S(1)}, u32[]{:S(2)}, u32[]{:S(2)}) collective-permute-start(f32[16,256]{1,0:T(8,128)S(1)} %pad_maximum_fusion.9), channel_id=1, source_target_pairs={{0,16},{16,0},{32,48},{48,32},{64,80},{80,64},{96,112},{112,96},{1... | collective-permute-start | bytes 49160 | tf_op jit(solution)/shard_map/ppermute | solution.py:35
  12.4 0.8 constant_dynamic-slice_fusion.2
  13.1 0.0 collective-permute-done
  13.2 0.7 slice_add_fusion.1
  13.9 27.8 %all-gather = f32[768,256]{1,0:T(8,128)S(1)} all-gather(f32[48,256]{1,0:T(8,128)S(1)} %pad_maximum_fusion.7), channel_id=2, replica_groups={{0,32,64,96,128,160,192,224,256,288,320,352,384,416,448,480},{16,48,80,..., dimensions={0}, use_global_device_ids=true | all-gather | bytes 835584 | tf_op jit(solution)/shard_map/all_gather | solution.py:52
  41.8 0.1 pad_maximum_fusion.3
  41.9 16.9 %all_to_all.15 = f32[16,48,256]{2,1,0:T(8,128)S(1)} all-to-all(f32[16,48,256]{2,1,0:T(8,128)S(1)} %pad_maximum_fusion.3), channel_id=1, replica_groups=mesh['row'=32,'col'=16] {'col'}, dimensions={0} | all-to-all | bytes 1572864 | tf_op jit(solution)/shard_map/all_to_all | solution.py:46
  58.8 10.3 %collective-permute-start.1 = (f32[16,48,256]{2,1,0:T(8,128)S(1)}, f32[16,48,256]{2,1,0:T(8,128)S(1)}, u32[]{:S(2)}, u32[]{:S(2)}) collective-permute-start(f32[16,48,256]{2,1,0:T(8,128)S(1)} %all_to_all.15), channel_id=1, source_target_pairs={{0,16},{16,0},{32,48},{48,32},{64,80},{80,64},{96,112},{112,96},{1... | collective-permute-start | bytes 2359304 | tf_op jit(solution)/shard_map/ppermute | solution.py:35
  69.1 1.9 %collective-permute-done.1 = f32[16,48,256]{2,1,0:T(8,128)S(1)} collective-permute-done((f32[16,48,256]{2,1,0:T(8,128)S(1)}, f32[16,48,256]{2,1,0:T(8,128)S(1)}, u32[]{:S(2)}, u32[]{:S(2)}) %collective-permute-start.1) | collective-permute-done | bytes 786464 | tf_op jit(solution)/shard_map/ppermute | solution.py:35
  71.0 0.1 broadcast_select_fusion.3
  71.2 0.1 pad_maximum_fusion.1
  71.3 0.8 pad_maximum_fusion.5
  72.1 15.5 %shard_map.41 = (f32[256,256]{1,0:T(8,128)}, f32[256,256]{1,0:T(8,128)}) custom-call(f32[256,256]{1,0:T(8,128)} %bitcast.58, f32[256,256]{1,0:T(8,128)} %bitcast.57), custom_call_target="tpu_custom_call" | custom-call | tf_op jit(solution)/shard_map/pallas_call | solution.py:141
  87.6 1.1 bitcast_add_fusion
  88.8 0.0 copy-start
  88.8 0.0 copy-start.3
  88.8 3.5 %fusion.8 = f32[256,512]{1,0:T(8,128)S(1)} fusion(f32[1024,256]{1,0:T(8,128)S(1)} %bitcast_add_fusion, f32[512,1024]{1,0:T(8,128)} %param.3), kind=kOutput, calls=%fused_computation.40 | convolution fusion | flops 805306368 | bytes 3670016 | tf_op jit(solution)/shard_map/dot_general | solution.py:15
  92.3 0.2 copy.7
  92.5 0.0 copy-done
  92.5 0.0 copy-done.3
  92.5 1.0 fusion
  93.5 0.1 pad_maximum_fusion.4
  93.6 16.4 %all_to_all.16 = f32[16,48,256]{2,1,0:T(8,128)S(1)} all-to-all(f32[16,48,256]{2,1,0:T(8,128)S(1)} %pad_maximum_fusion.4), channel_id=1, replica_groups=mesh['row'=32,'col'=16] {'col'}, dimensions={0} | all-to-all | bytes 1572864 | tf_op jit(solution)/shard_map/all_to_all | solution.py:193
  110.0 0.1 reduce_sum.28
  110.1 24.1 %all-gather.1 = f32[768,256]{1,0:T(8,128)S(1)} all-gather(f32[48,256]{1,0:T(8,128)S(1)} %reduce_sum.28), channel_id=3, replica_groups={{0,32,64,96,128,160,192,224,256,288,320,352,384,416,448,480},{16,48,80,..., dimensions={0}, use_global_device_ids=true | all-gather | bytes 835584 | tf_op jit(solution)/shard_map/all_gather | solution.py:52
  134.3 0.1 broadcast_in_dim.23
  134.4 0.1 pad_maximum_fusion
  134.5 16.9 %all_to_all.17 = f32[16,80,256]{2,1,0:T(8,128)S(1)} all-to-all(f32[16,80,256]{2,1,0:T(8,128)S(1)} %pad_maximum_fusion), channel_id=1, replica_groups=mesh['row'=32,'col'=16] {'col'}, dimensions={0} | all-to-all | bytes 2621440 | tf_op jit(solution)/shard_map/all_to_all | solution.py:46
  151.4 0.0 copy-start.2
  151.4 0.1 slice.85
  151.4 11.0 %collective-permute-start.2 = (f32[16,48,256]{2,1,0:T(8,128)S(1)}, f32[16,48,256]{2,1,0:T(8,128)S(1)}, u32[]{:S(2)}, u32[]{:S(2)}) collective-permute-start(f32[16,48,256]{2,1,0:T(8,128)S(1)} %slice.85), channel_id=1, source_target_pairs={{0,16},{16,0},{32,48},{48,32},{64,80},{80,64},{96,112},{112,96},{1... | collective-permute-start | bytes 2359304 | tf_op jit(solution)/shard_map/ppermute | solution.py:35
  162.5 0.7 neg.3
  163.2 0.0 copy-done.2
  163.2 0.4 fusion.9
  163.6 1.0 fusion.10
  164.7 0.0 collective-permute-done.2
  164.7 0.1 broadcast_select_fusion.1
  165.0 0.4 fusion.12
  165.3 0.6 fusion.13
  165.9 0.1 pad_maximum_fusion.2
  166.0 0.6 fusion.11
  166.6 0.0 copy-start.1
  166.6 0.6 convolution_subtract_fusion
  167.2 1.0 copy-done.1
  168.2 2.6 %subtract_subtract_fusion = f32[512,1024]{1,0:T(8,128)} fusion(f32[512,1024]{1,0:T(8,128)S(1)} %copy-done.1, f32[512,1024]{1,0:T(8,128)S(1)} %fusion.10, f32[1024,256]{1,0:T(8,128)S(1)} %convolution_subtract_fusion, f32[512,256]{1,0:T(8,128)S(1)} %copy-done, f32[256,256]{1,0:T(8,128)S(1)} %copy-done.3, pred[]{:T(512)S(6)} %eq.17), kind=kOutput, calls=%fused_computation | convolution fusion | flops 806617088 | bytes 8126465 | tf_op jit(solution)/shard_map/dot_general | solution.py:19
  (17 shorter events, 0.4 us)
Async XLA Ops:
  3.6 9.6 %collective-permute-start = (f32[16,256]{1,0:T(8,128)S(1)}, f32[16,256]{1,0:T(8,128)S(1)}, u32[]{:S(2)}, u32[]{:S(2)}) collective-permute-start(f32[16,256]{1,0:T(8,128)S(1)} %pad_maximum_fusion.9), channel_id=1, source_target_pairs={{0,16},{16,0},{32,48},{48,32},{64,80},{80,64},{96,112},{112,96},{1... | collective-permute-start | bytes 49160 | tf_op jit(solution)/shard_map/ppermute | solution.py:35
  58.8 12.2 %collective-permute-start.1 = (f32[16,48,256]{2,1,0:T(8,128)S(1)}, f32[16,48,256]{2,1,0:T(8,128)S(1)}, u32[]{:S(2)}, u32[]{:S(2)}) collective-permute-start(f32[16,48,256]{2,1,0:T(8,128)S(1)} %all_to_all.15), channel_id=1, source_target_pairs={{0,16},{16,0},{32,48},{48,32},{64,80},{80,64},{96,112},{112,96},{1... | collective-permute-start | bytes 2359304 | tf_op jit(solution)/shard_map/ppermute | solution.py:35
  88.8 3.7 %copy-start = (f32[512,256]{1,0:T(8,128)S(1)}, f32[512,256]{1,0:T(8,128)}, u32[]{:S(2)}) copy-start(f32[512,256]{1,0:T(8,128)} %param.2) | copy-start | bytes 1572868
  88.8 3.7 %copy-start.3 = (f32[256,256]{1,0:T(8,128)S(1)}, f32[256,256]{1,0:T(8,128)}, u32[]{:S(2)}) copy-start(f32[256,256]{1,0:T(8,128)} %get-tuple-element.4) | copy-start | bytes 786436
  151.4 11.9 %copy-start.2 = (f32[256,256]{1,0:T(8,128)S(1)}, f32[256,256]{1,0:T(8,128)}, u32[]{:S(2)}) copy-start(f32[256,256]{1,0:T(8,128)} %get-tuple-element.5) | copy-start | bytes 786436
  151.4 13.3 %collective-permute-start.2 = (f32[16,48,256]{2,1,0:T(8,128)S(1)}, f32[16,48,256]{2,1,0:T(8,128)S(1)}, u32[]{:S(2)}, u32[]{:S(2)}) collective-permute-start(f32[16,48,256]{2,1,0:T(8,128)S(1)} %slice.85), channel_id=1, source_target_pairs={{0,16},{16,0},{32,48},{48,32},{64,80},{80,64},{96,112},{112,96},{1... | collective-permute-start | bytes 2359304 | tf_op jit(solution)/shard_map/ppermute | solution.py:35
  166.6 1.6 copy-start.1
